TPU v7x, 256 devices: a whole 4x4x8 slice. The times are simulated.
256 devices in a mesh: ctx: 64 (over x, z, y_hi), tp: 4 (over y_lo, core).
Axes of the slice: x: 4, y: 4 (y_hi: 2, y_lo: 2; y = y_hi * 2 + y_lo), z: 8, core: 2. Of those that a mesh axis runs over, the one named last changes fastest.
Arguments:
- tokens: bfloat16 [16384, 8192], P('ctx'), may hold values from -6 to 6
- select_index: int32 [2048], P('ctx'), may hold values from 0 to 255, as said below
- valid_count: int32 [64], replicated, may hold values from 4 to 32, as said below
- queries: bfloat16 [2048, 4096], P('ctx', 'tp'), may hold values from -160 to 160
- key_matrix: bfloat16 [8192, 512], P('ctx', 'tp'), may hold values from -0.0625 to 0.0625
- value_matrix: bfloat16 [8192, 512], P('ctx', 'tp'), may hold values from -0.0625 to 0.0625
- out_grad: bfloat16 [2048, 4096], P('ctx', 'tp'), may hold values from -6 to 6
Outputs:
- attended: bfloat16 [2048, 4096], P('ctx', 'tp')
- query_gradient: bfloat16 [2048, 4096], P('ctx', 'tp')
- token_grad: bfloat16 [16384, 8192], P('ctx', 'tp')
- key_weight_grad: bfloat16 [8192, 512], P('ctx', 'tp')
- value_weight_grad: bfloat16 [8192, 512], P('ctx', 'tp')
Inputs may be any that keep to these rules, and one draw needn't show every extreme that they name: `select_index`: within one shard the offsets of all 32 slots are distinct, and those of the first valid_count slots rise. `valid_count`: some shard holds exactly 32 live slots.
All inputs are finite; a program needn't handle non-finite values.
Results may differ from a plain program's by a relative error of at most 0.023.
The roundings to bfloat16 on the way count: a program that leaves them out, or rounds other values in their place, can miss the bound.
Values may be sent and summed in bfloat16 or wider, within the bound.
A program may use at most 64 MiB of HBM per device.

v0:
```python
import math

import jax
import jax.numpy as jnp
from jax import lax
from jax.sharding import PartitionSpec as P

HEAD_WIDTH = 128


neg_large = -1e30


def local(tokens, select_index, valid_count, queries, key_matrix, value_matrix, out_grad):
    shard_len = tokens.shape[0]
    capacity = select_index.shape[0]
    key_value_width = key_matrix.shape[1]
    kv_local = key_value_width // HEAD_WIDTH
    per_group = queries.shape[1] // key_value_width
    ctx_size = lax.axis_size("ctx")
    own_shard = lax.axis_index("ctx")
    all_keys = ctx_size * capacity
    block_len = min(512, all_keys)
    num_blocks = all_keys // block_len
    score_scale = 1.0 / math.sqrt(HEAD_WIDTH)
    slot_ids = jnp.arange(capacity, dtype=jnp.int32)
    own_count = jnp.sum(
        jnp.where(jnp.arange(ctx_size, dtype=jnp.int32) == own_shard, valid_count, 0)
    )
    live_query = slot_ids < own_count
    query_pos = jnp.where(live_query, select_index, shard_len)
    key_shard = jnp.arange(all_keys, dtype=jnp.int32) // capacity
    key_live = (slot_ids[None, :] < valid_count[:, None]).reshape(all_keys)
    key_pos = jnp.tile(select_index, ctx_size)
    picked = jnp.take(tokens, select_index, axis=0)
    weight_key, weight_value = (
        lax.all_gather(key_matrix, "ctx", axis=0, tiled=True),
        lax.all_gather(value_matrix, "ctx", axis=0, tiled=True),
    )
    both_weights = jnp.concatenate([weight_key, weight_value], axis=1)
    projected = jnp.dot(picked, both_weights, preferred_element_type=jnp.float32).astype(
        jnp.bfloat16
    )
    kv_rows = lax.all_gather(projected, "ctx", axis=0, tiled=True)
    heads_of_query = queries.reshape(capacity, kv_local, per_group, HEAD_WIDTH)
    gradient_rows = jnp.where(live_query[:, None], out_grad, jnp.zeros_like(out_grad))
    gradient_heads = gradient_rows.reshape(capacity, kv_local, per_group, HEAD_WIDTH)
    stat_shape = (kv_local, per_group, capacity)

    def block_data(blk_id):
        leading_item = blk_id * block_len
        kv_blk = lax.dynamic_slice_in_dim(kv_rows, leading_item, block_len, 0)
        key_block = kv_blk[:, :key_value_width].reshape(block_len, kv_local, HEAD_WIDTH)
        value_block = kv_blk[:, key_value_width:].reshape(block_len, kv_local, HEAD_WIDTH)
        live_blk = lax.dynamic_slice_in_dim(key_live, leading_item, block_len, 0)
        shard_blk = lax.dynamic_slice_in_dim(key_shard, leading_item, block_len, 0)
        pos_blk = lax.dynamic_slice_in_dim(key_pos, leading_item, block_len, 0)
        same_shard = (shard_blk[None, :] == own_shard) & (pos_blk[None, :] <= query_pos[:, None])
        visible = live_blk[None, :] & ((shard_blk[None, :] < own_shard) | same_shard)
        active = leading_item // capacity <= own_shard
        return (key_block, value_block, visible, active)

    def block_scores(key_block, visible):
        scores = (
            jnp.einsum(
                "toul,iol->outi", heads_of_query, key_block, preferred_element_type=jnp.float32
            )
            * score_scale
        )
        return jnp.where(visible[None, None], scores, neg_large)

    def max_step(carried, blk_id):
        row_max, row_sum = carried
        key_block, value_block, visible, active = block_data(blk_id)

        def max_visit():
            scores = block_scores(key_block, visible)
            new_max = jnp.maximum(row_max, jnp.max(scores, axis=-1))
            terms = jnp.where(visible[None, None], jnp.exp(scores - new_max[..., None]), 0.0)
            new_sum = row_sum * jnp.exp(row_max - new_max) + jnp.sum(terms, axis=-1)
            return ((new_max, new_sum), scores)

        def max_ignore():
            return ((row_max, row_sum), jnp.full(stat_shape + (block_len,), neg_large, jnp.float32))

        stats, scores = lax.cond(active, max_visit, max_ignore)
        return (stats, None)

    start_stats = (jnp.full(stat_shape, neg_large, jnp.float32), jnp.zeros(stat_shape, jnp.float32))
    block_ids = jnp.arange(num_blocks, dtype=jnp.int32)
    (row_max, row_sum), stored = lax.scan(max_step, start_stats, block_ids)
    log_total = row_max + jnp.log(row_sum)

    def get_scores(key_block, visible):
        return block_scores(key_block, visible)

    def out_step(output_acc, blk_id):
        key_block, value_block, visible, active = block_data(blk_id)

        def out_visit():
            probs = jnp.exp(get_scores(key_block, visible) - log_total[..., None])
            weight_matrices = probs.astype(jnp.bfloat16)
            return output_acc + jnp.einsum(
                "ljvo,olf->vljf", weight_matrices, value_block, preferred_element_type=jnp.float32
            )

        def out_ignore():
            return output_acc

        return (lax.cond(active, out_visit, out_ignore), None)

    head_shape = (capacity, kv_local, per_group, HEAD_WIDTH)
    output_acc, unused = lax.scan(out_step, jnp.zeros(head_shape, jnp.float32), block_ids)
    attended = jnp.where(live_query[:, None, None, None], output_acc, 0.0).astype(jnp.bfloat16)
    out_dot = jnp.transpose(
        jnp.sum(gradient_heads.astype(jnp.float32) * attended.astype(jnp.float32), axis=-1),
        (1, 2, 0),
    )

    def grad_step(query_acc, blk_id):
        key_block, value_block, visible, active = block_data(blk_id)

        def grad_visit():
            probs = jnp.exp(get_scores(key_block, visible) - log_total[..., None])
            weight_matrices = probs.astype(jnp.bfloat16)
            grad_probs = jnp.einsum(
                "toul,iol->outi", gradient_heads, value_block, preferred_element_type=jnp.float32
            )
            score_gradient = (probs * (grad_probs - out_dot[..., None]) * score_scale).astype(
                jnp.bfloat16
            )
            new_acc = query_acc + jnp.einsum(
                "ljvo,olf->vljf", score_gradient, key_block, preferred_element_type=jnp.float32
            )
            key_part = jnp.einsum(
                "cifh,fcij->hcj", score_gradient, heads_of_query, preferred_element_type=jnp.float32
            )
            value_part = jnp.einsum(
                "cifh,fcij->hcj",
                weight_matrices,
                gradient_heads,
                preferred_element_type=jnp.float32,
            )
            return (
                new_acc,
                jnp.concatenate(
                    [
                        key_part.reshape(block_len, key_value_width),
                        value_part.reshape(block_len, key_value_width),
                    ],
                    axis=1,
                ),
            )

        def grad_ignore():
            return (query_acc, jnp.zeros((block_len, 2 * key_value_width), jnp.float32))

        return lax.cond(active, grad_visit, grad_ignore)

    query_acc, kv_terms = lax.scan(grad_step, jnp.zeros(head_shape, jnp.float32), block_ids)
    query_gradient = query_acc.astype(jnp.bfloat16).reshape(
        capacity, kv_local * per_group * HEAD_WIDTH
    )
    kv_terms = kv_terms.reshape(all_keys, 2 * key_value_width)
    own_grads = lax.psum_scatter(kv_terms, "ctx", scatter_dimension=0, tiled=True).astype(
        jnp.bfloat16
    )
    weight_grad = lax.psum_scatter(
        lax.dot_general(
            picked, own_grads, (((0,), (0,)), ((), ())), preferred_element_type=jnp.float32
        ),
        "ctx",
        scatter_dimension=0,
        tiled=True,
    )
    key_weight_grad = weight_grad[:, :key_value_width].astype(jnp.bfloat16)
    value_weight_grad = weight_grad[:, key_value_width:].astype(jnp.bfloat16)
    row_grad = lax.dot_general(
        own_grads, both_weights, (((1,), (1,)), ((), ())), preferred_element_type=jnp.float32
    )
    summed = lax.psum_scatter(row_grad, "tp", scatter_dimension=1, tiled=True)
    summed = jnp.where(live_query[:, None], summed, 0.0)
    token_grad = (
        jnp.zeros((shard_len, summed.shape[1]), jnp.float32)
        .at[select_index]
        .set(summed)
        .astype(jnp.bfloat16)
    )
    return (
        attended.reshape(capacity, kv_local * per_group * HEAD_WIDTH),
        query_gradient,
        token_grad,
        key_weight_grad,
        value_weight_grad,
    )


def solution(mesh):
    in_specs = (
        P("ctx", None),
        P("ctx"),
        P(),
        P("ctx", "tp"),
        P("ctx", "tp"),
        P("ctx", "tp"),
        P("ctx", "tp"),
    )
    out_specs = (P("ctx", "tp"), P("ctx", "tp"), P("ctx", "tp"), P("ctx", "tp"), P("ctx", "tp"))
    return jax.shard_map(local, mesh=mesh, in_specs=in_specs, out_specs=out_specs, check_vma=False)
```

profile of v0, /device:TPU:8, one launch (start us, length us, event | category | flops | bytes accessed | tf_op | source)
XLA Modules:
  0.0 1205.8 jit_solution(602995603653789307)
XLA Ops:
  7.2 0.7 all-gather.4.cloned.1.call-update
  7.9 0.7 all-gather.6.cloned.1.call-update
  8.7 1.3 fusion.76
  10.0 1.2 broadcast_select_fusion.3
  11.2 4.1 gather_fusion
  15.3 116.2 %all-gather.4.cloned.1.call-done = bf16[8192,128]{1,0:T(8,128)(2,1)} async-done(((bf16[128,128]{1,0:T(8,128)(2,1)}), bf16[8192,128]{1,0:T(8,128)(2,1)}) %all-gather.4.cloned.1.call-update) | async-done | bytes 2097168 | tf_op jit(solution)/shard_map/all_gather | solution.py:37
  131.5 3.2 constant_dynamic-update-slice_fusion.2
  134.7 114.9 %all-gather.6.cloned.1.call-done = bf16[8192,128]{1,0:T(8,128)(2,1)} async-done(((bf16[128,128]{1,0:T(8,128)(2,1)}), bf16[8192,128]{1,0:T(8,128)(2,1)}) %all-gather.6.cloned.1.call-update) | async-done | bytes 2097168 | tf_op jit(solution)/shard_map/all_gather | solution.py:38
  249.6 3.1 constant_dynamic-update-slice_fusion.1
  252.7 3.7 convolution_convert_fusion
  257.2 110.9 %all-gather.8.cloned.1.call-done = bf16[2048,256]{1,0:T(8,128)(2,1)} async-done(((bf16[32,256]{1,0:T(8,128)(2,1)}), bf16[2048,256]{1,0:T(8,128)(2,1)}) %all-gather.8.cloned.1.call-update) | async-done | bytes 1048592 | tf_op jit(solution)/shard_map/all_gather | solution.py:44
  368.1 7.5 while.49
  368.2 0.6 dynamic_slice.201
  369.5 2.1 conditional.9
  370.1 1.2 fusion.80
  371.6 0.6 dynamic_slice.201
  373.0 0.6 dynamic_slice.201
  374.3 0.6 dynamic_slice.201
  375.7 7.3 while.50
  375.7 0.6 dynamic_slice.202
  377.0 2.0 conditional.10
  377.6 1.4 fusion.31
  379.0 0.6 dynamic_slice.202
  380.3 0.6 dynamic_slice.202
  381.7 0.6 dynamic_slice.202
  383.3 14.4 %while.51 = (s32[]{:T(128)}, f32[32,1,8,128]{3,0,2,1:T(8,128)S(1)}, f32[4,512,256]{2,1,0:T(8,128)}, s32[4]{0:T(128)S(1)}, s32[]{:T(128)}, /*index=5*/bf16[2048,2...) while((s32[]{:T(128)}, f32[32,1,8,128]{3,0,2,1:T(8,128)S(1)}, ...), condition=%wide.region_15.16_spmd.clone, body=%wide.region_12.15_spmd.clone.sunk | while | flops 169058832 | bytes 7068294 | solution.py:160
  383.3 0.6 dynamic_slice.203
  384.6 4.7 conditional.11
  385.2 1.2 fusion.52
  386.4 1.2 fusion.53
  387.6 1.2 fusion.54
  389.5 0.8 constant_dynamic-update-slice_fusion.4
  390.4 0.6 dynamic_slice.203
  392.0 0.8 constant_dynamic-update-slice_fusion.4
  392.8 0.6 dynamic_slice.203
  394.4 0.9 constant_dynamic-update-slice_fusion.4
  395.3 0.6 dynamic_slice.203
  396.9 0.8 constant_dynamic-update-slice_fusion.4
  397.8 392.4 %reduce-scatter.4.cloned.1.call-done = f32[32,256]{1,0:T(8,128)} async-done(((f32[2048,256]{1,0:T(8,128)}), f32[32,256]{1,0:T(8,128)}) %reduce-scatter.4.cloned.1.call-update) | async-done | bytes 32784 | tf_op jit(solution)/shard_map/reduce_scatter | solution.py:165
  790.2 4.5 fusion.74
  794.8 4.6 fusion.69
  799.5 0.7 copy_bitcast_fusion
  800.2 9.3 reduce-scatter.6.cloned.1.call-done
  809.4 1.8 scatter_custom_fusion
  811.2 1.1 convert_element_type.73
  812.3 385.1 %reduce-scatter.8.cloned.1.call-done = f32[128,256]{1,0:T(8,128)} async-done(((f32[8192,256]{1,0:T(8,128)}), f32[128,256]{1,0:T(8,128)}) %reduce-scatter.8.cloned.1.call-update) | async-done | bytes 131088 | tf_op jit(solution)/shard_map/reduce_scatter | solution.py:168
  1197.4 0.9 convert.4
  1198.4 0.6 fusion.81
  (127 shorter events, 5.3 us)
Async XLA Ops:
  7.2 124.3 %all-gather.4.cloned.1.call-start = ((), (), s32[]{:S(2)}) async-start(), calls=%async_computation.3 | async-start | bytes 2129920 | tf_op jit(solution)/shard_map/all_gather | solution.py:37
  7.9 241.7 %all-gather.6.cloned.1.call-start = ((), (), s32[]{:S(2)}) async-start(), calls=%async_computation.4 | async-start | bytes 2129920 | tf_op jit(solution)/shard_map/all_gather | solution.py:38
  8.7 359.5 %all-gather.8.cloned.1.call-start = ((), (), s32[]{:S(2)}) async-start(), calls=%async_computation.5 | async-start | bytes 1064960 | tf_op jit(solution)/shard_map/all_gather | solution.py:44
  11.2 4.1 copy-start.1
  252.7 4.4 copy-start.3
  252.7 4.5 copy-start.4
  252.7 115.4 %copy-start.2 = (s32[64]{0:T(128)S(1)}, s32[64]{0:T(128)}, u32[]{:S(2)}) copy-start(s32[64]{0:T(128)} %param.21) | copy-start | bytes 772
  256.4 533.8 %reduce-scatter.4.cloned.1.call-start = ((), (), s32[]{:S(2)}) async-start(), calls=%async_computation.6 | async-start | bytes 2129920 | tf_op jit(solution)/shard_map/reduce_scatter | solution.py:165
  397.7 411.7 %reduce-scatter.6.cloned.1.call-start = ((), (), s32[]{:S(2)}) async-start(), calls=%async_computation.7 | async-start | bytes 1310720 | tf_op jit(solution)/shard_map/reduce_scatter | solution.py:181
  790.2 4.6 copy-start
  794.7 402.7 %reduce-scatter.8.cloned.1.call-start = ((), (), s32[]{:S(2)}) async-start(), calls=%async_computation.8 | async-start | bytes 8519680 | tf_op jit(solution)/shard_map/reduce_scatter | solution.py:168
Sparse Core Ops, SparseCore 0:
  11.6 119.8 all-gather.3
  135.1 114.4 all-gather.5
  256.5 111.5 all-gather.7
  397.9 392.2 reduce-scatter.3
  794.9 14.5 reduce-scatter.5
  811.8 385.5 reduce-scatter.7
where the time goes:
time: 1210 us
  waiting for transfers between devices  1130 us (93%)
  local copies, waits for them, and re-layouts  24.3 us (2%)
  matrix products  19.4 us (2%)
  between operations  14.3 us (1%)
    reduce_scatter x1, waiting for transfers between devices, local(): lax.psum_scatter(kv_terms, 'ctx', scatter_dimension=0, tiled=True)  392 us
    reduce_scatter x1, waiting for transfers between devices, local(): lax.psum_scatter(lax.dot_general(picked, own_grads, (((0,), (0,)), ((), (...  385 us
    all_gather x1, waiting for transfers between devices, local(): lax.all_gather(key_matrix, 'ctx', axis=0, tiled=True)  116 us
    all_gather x1, waiting for transfers between devices, local(): lax.all_gather(value_matrix, 'ctx', axis=0, tiled=True)  115 us
    all_gather x1, waiting for transfers between devices, local(): kv_rows = lax.all_gather(projected, 'ctx', axis=0, tiled=True)  111 us
  transfers between devices with their start and end apart: 6, of which 6 were waited for; matrix products, arithmetic and copies ran while one was open for 2% of the time, Pallas kernels for 0%

commit v1 on v0

v1 whole, which is shorter than its diff:
```python
import math

import jax
import jax.numpy as jnp
from jax import lax
from jax.experimental import pallas as pl
from jax.experimental.pallas import tpu as pltpu
from jax.sharding import PartitionSpec as P

NX, NZ, NY = 4, 8, 2
HEAD = 128
SLOTS = 32
KV = 2 * HEAD
HEADS = 8
ROWS = 256
MODEL = 8192
PER_X = NZ * NY
CHUNK = PER_X * SLOTS
QROWS = HEADS * SLOTS
SCALE = 1.0 / math.sqrt(HEAD)
NEG = -1e30
BF = jnp.bfloat16
F32 = jnp.float32
ZORDER = (4, 3, 5, 2, 6, 1, 7)
ARRIVE = (1, 7, 2, 6, 3, 5, 4)


def dot(a, b, ca, cb):
    return lax.dot_general(a, b, (((ca,), (cb,)), ((), ())), preferred_element_type=F32)


def kernel(
    tok_hbm, sel_ref, vc_ref, q_ref, wk_ref, wv_ref, g_ref,
    att_ref, dq_ref, tg_ref, kwg_ref, vwg_ref,
    tok, pz, xz, wg, pf, pr, kv, s_ref, qs, gs, tf, tb, hl, hr, cl, cr, ub, zr, vs, yr, gz,
    wb, wf, whl, whr, wcl, wcr, wyb, wyr, rsb, rsr, rf, ryb, ryr, tz, tr,
    tok_sem, z_send, z_recv, x_send, x_recv, ag_send, ag_recv,
):
    c = lax.axis_index("ctx")
    t = lax.axis_index("tp")
    x = c // PER_X
    z = (c // NY) % NZ
    y = c % NY
    core = t % 2
    ylo = t // 2
    right = (x + 1) % NX
    left = (x + NX - 1) % NX

    def at(xx, zz, yy):
        return {"ctx": (xx * NZ + zz) * NY + yy, "tp": t}

    def zpeer(d):
        return at(x, (z + d) % NZ, y)

    to_right = at(right, z, y)
    to_left = at(left, z, y)
    to_y = at(x, z, 1 - y)
    to_sib = {"ctx": c, "tp": 2 * ylo + 1 - core}
    to_ylo = {"ctx": c, "tp": 2 * (1 - ylo) + core}

    started = []

    def copy(src, dst, ssem, rsem, dev):
        return pltpu.make_async_remote_copy(
            src_ref=src, dst_ref=dst, send_sem=ssem, recv_sem=rsem,
            device_id=dev, device_id_type=pl.DeviceIdType.MESH,
        )

    def send(src, dst, ssem, rsem, dev):
        cp = copy(src, dst, ssem, rsem, dev)
        cp.start()
        started.append(cp)

    def arrived(dst, rsem, dev):
        copy(dst, dst, rsem, rsem, dev).wait_recv()

    half_cols = 2 * NZ * KV
    tok_cp = pltpu.make_async_copy(
        tok_hbm.at[:, pl.ds(pl.multiple_of(core * half_cols, half_cols), half_cols)], tok, tok_sem
    )
    tok_cp.start()

    barrier = pltpu.get_barrier_semaphore()
    partners = [zpeer(d) for d in range(1, NZ)] + [to_right, to_left, to_y, to_sib, to_ylo]
    for dev in partners:
        pl.semaphore_signal(barrier, inc=1, device_id=dev, device_id_type=pl.DeviceIdType.MESH)

    wg[x, y, :, 0:HEAD] = wk_ref[...]
    wg[x, y, :, HEAD:KV] = wv_ref[...]

    sel_row = jnp.broadcast_to(sel_ref[...], (SLOTS, SLOTS))
    i0 = lax.broadcasted_iota(jnp.int32, (SLOTS, SLOTS), 0)
    i1 = lax.broadcasted_iota(jnp.int32, (SLOTS, SLOTS), 1)
    sel_col = jnp.sum(jnp.where(i0 == i1, sel_row, 0), axis=1, keepdims=True)
    hot = jnp.where(
        lax.broadcasted_iota(jnp.int32, (SLOTS, ROWS), 1) == sel_col, 1.0, 0.0
    ).astype(BF)
    vc = vc_ref[...]
    own_count = jnp.sum(
        jnp.where(lax.broadcasted_iota(jnp.int32, vc.shape, 1) == c, vc, 0), axis=1, keepdims=True
    )
    live_col = lax.broadcasted_iota(jnp.int32, (SLOTS, 1), 0) < own_count
    live = jnp.where(live_col, 1.0, 0.0)
    qpos = jnp.where(live_col, sel_col, ROWS).astype(F32)
    qpos_all = jnp.concatenate([qpos] * HEADS, axis=0)
    for h in range(HEADS):
        qs[h * SLOTS:(h + 1) * SLOTS, :] = q_ref[:, h * HEAD:(h + 1) * HEAD]
        gs[h * SLOTS:(h + 1) * SLOTS, :] = (
            g_ref[:, h * HEAD:(h + 1) * HEAD].astype(F32) * live
        ).astype(BF)

    pl.semaphore_wait(barrier, len(partners))

    ws, wr = x_send.at[0], x_recv.at[0]
    send(wg.at[x, y], wg.at[x, y], ws.at[0], wr.at[0], to_y)
    send(wg.at[x, y], wg.at[x, y], ws.at[1], wr.at[1], to_right)
    send(wg.at[x, y], wg.at[x, y], ws.at[2], wr.at[2], to_left)

    tok_cp.wait()
    for zt in range(NZ):
        for k in range(2):
            c0 = k * NZ * KV + zt * KV
            pz[zt, k] = dot(hot, tok[:, c0:c0 + KV], 1, 0).astype(BF)
    for d in ZORDER:
        send(
            pz.at[(z + d) % NZ], xz.at[pl.ds(2 * core, 2), z],
            z_send.at[0, d], z_recv.at[0, d], zpeer(d),
        )
    xz[pl.ds(2 * core, 2), z] = pz[z]
    send(
        pz.at[z], xz.at[pl.ds(2 * core, 2), z], z_send.at[1, 0], z_recv.at[1, 0], to_sib
    )

    arrived(wg.at[x, 1 - y], wr.at[0], to_y)
    send(wg.at[x, 1 - y], wg.at[x, 1 - y], ws.at[3], wr.at[3], to_right)
    send(wg.at[x, 1 - y], wg.at[x, 1 - y], ws.at[4], wr.at[4], to_left)

    for d in ARRIVE:
        zs = (z + NZ - d) % NZ
        mine = xz.at[pl.ds(2 * core, 2), zs]
        arrived(mine, z_recv.at[0, d], zpeer(d))
        send(mine, mine, z_send.at[1, d], z_recv.at[1, d], to_sib)

    arrived(wg.at[left, y], wr.at[1], to_left)
    arrived(wg.at[left, 1 - y], wr.at[3], to_left)
    send(wg.at[left, 0], wg.at[left, 0], ws.at[5], wr.at[5], to_right)
    arrived(wg.at[right, y], wr.at[2], to_right)
    arrived(wg.at[right, 1 - y], wr.at[4], to_right)
    send(wg.at[right, 1], wg.at[right, 1], ws.at[6], wr.at[6], to_left)
    for d in (0,) + ARRIVE:
        zs = (z + NZ - d) % NZ
        arrived(xz.at[pl.ds(2 * (1 - core), 2), zs], z_recv.at[1, d], to_sib)
    far = (x + 2) % NX
    arrived(wg.at[far, 0], wr.at[5], to_left)
    arrived(wg.at[far, 1], wr.at[6], to_right)

    acc = jnp.zeros((NZ * SLOTS, KV), F32)
    for xx in range(NX):
        acc = acc + dot(
            xz[xx].reshape(NZ * SLOTS, KV), wg[xx].reshape(NY * HEAD, KV), 1, 0
        )
    pf[...] = acc.reshape(NZ, SLOTS, KV)
    for d in ZORDER:
        send(pf.at[(z + d) % NZ], pr.at[z], z_send.at[2, d], z_recv.at[2, d], zpeer(d))
    total = pf[z]
    for d in ARRIVE:
        zs = (z + NZ - d) % NZ
        arrived(pr.at[zs], z_recv.at[2, d], zpeer(d))
        total = total + pr[zs]
    kv[c] = total.astype(BF)

    send(kv.at[c], kv.at[c], z_send.at[3, 0], z_recv.at[3, 0], to_y)
    peer_c = (x * NZ + z) * NY + 1 - y
    arrived(kv.at[peer_c], z_recv.at[3, 0], to_y)

    def pair(xx, zz):
        return kv.at[pl.ds((xx * NZ + zz) * NY, NY)]

    def one(xx, zz, yy):
        return kv.at[(xx * NZ + zz) * NY + yy]

    for d in ZORDER:
        send(pair(x, z), pair(x, z), z_send.at[3, d], z_recv.at[3, d], zpeer(d))
    for d in (0,) + ARRIVE:
        zs = (z + NZ - d) % NZ
        if d:
            arrived(pair(x, zs), z_recv.at[3, d], zpeer(d))
        send(pair(x, zs), pair(x, zs), ag_send.at[0, d], ag_recv.at[0, d], to_right)
        send(pair(x, zs), pair(x, zs), ag_send.at[1, d], ag_recv.at[1, d], to_left)
    for d in (0,) + ARRIVE:
        zs = (z + NZ - d) % NZ
        arrived(pair(left, zs), ag_recv.at[0, d], to_left)
        send(one(left, zs, 0), one(left, zs, 0), ag_send.at[2, d], ag_recv.at[2, d], to_right)
        arrived(pair(right, zs), ag_recv.at[1, d], to_right)
        send(one(right, zs, 1), one(right, zs, 1), ag_send.at[3, d], ag_recv.at[3, d], to_left)
    for d in (0,) + ARRIVE:
        zs = (z + NZ - d) % NZ
        arrived(one(far, zs, 0), ag_recv.at[2, d], to_left)
        arrived(one(far, zs, 1), ag_recv.at[3, d], to_right)

    vc8 = jnp.broadcast_to(vc.astype(F32), (8, NX * PER_X)).astype(BF)
    sel8 = jnp.broadcast_to(sel_ref[...].astype(F32), (8, SLOTS)).astype(BF)
    jslot = lax.broadcasted_iota(jnp.int32, (SLOTS, CHUNK), 1) % SLOTS
    spread = jnp.where(jslot == lax.broadcasted_iota(jnp.int32, (SLOTS, CHUNK), 0), 1.0, 0.0)
    sel_keys = dot(sel8, spread.astype(BF), 1, 0)[0:1]
    queries = qs[...]
    grads = gs[...]

    def chunk_of(r):
        return (x + r) % NX

    def keys_of(r):
        return kv[pl.ds(chunk_of(r) * PER_X, PER_X), :, 0:HEAD].reshape(CHUNK, HEAD)

    def values_of(r):
        return kv[pl.ds(chunk_of(r) * PER_X, PER_X), :, HEAD:KV].reshape(CHUNK, HEAD)

    top = jnp.full((QROWS, 1), NEG, F32)
    for r in range(NX):
        shard = chunk_of(r) * PER_X + lax.broadcasted_iota(
            jnp.int32, (NX * PER_X, CHUNK), 1
        ) // SLOTS
        expand = jnp.where(
            shard == lax.broadcasted_iota(jnp.int32, (NX * PER_X, CHUNK), 0), 1.0, 0.0
        )
        counts = dot(vc8, expand.astype(BF), 1, 0)[0:1]
        shard_row = chunk_of(r) * PER_X + lax.broadcasted_iota(jnp.int32, (1, CHUNK), 1) // SLOTS
        slot_row = (lax.broadcasted_iota(jnp.int32, (1, CHUNK), 1) % SLOTS).astype(F32)
        place = jnp.where(shard_row < c, -1.0, jnp.where(shard_row > c, 1e6, sel_keys))
        place = jnp.where(slot_row < counts, place, 1e6)
        scores = dot(queries, keys_of(r), 1, 1) * SCALE
        scores = jnp.where(place <= qpos_all, scores, NEG)
        s_ref[:, r * CHUNK:(r + 1) * CHUNK] = scores
        top = jnp.maximum(top, jnp.max(scores, axis=1, keepdims=True))
    norm = jnp.zeros((QROWS, 1), F32)
    for r in range(NX):
        terms = jnp.exp(s_ref[:, r * CHUNK:(r + 1) * CHUNK] - top)
        s_ref[:, r * CHUNK:(r + 1) * CHUNK] = terms
        norm = norm + jnp.sum(terms, axis=1, keepdims=True)
    inv = 1.0 / norm
    out = jnp.zeros((QROWS, HEAD), F32)
    for r in range(NX):
        probs = s_ref[:, r * CHUNK:(r + 1) * CHUNK] * inv
        s_ref[:, r * CHUNK:(r + 1) * CHUNK] = probs
        out = out + dot(probs.astype(BF), values_of(r), 1, 0)
    live_all = jnp.concatenate([live] * HEADS, axis=0)
    attended = (out * live_all).astype(BF)
    for h in range(HEADS):
        att_ref[:, h * HEAD:(h + 1) * HEAD] = attended[h * SLOTS:(h + 1) * SLOTS]
    out_dot = jnp.sum(grads.astype(F32) * attended.astype(F32), axis=1, keepdims=True)

    dq = jnp.zeros((QROWS, HEAD), F32)
    es, er = x_send.at[1], x_recv.at[1]
    for r in (2, 1, 3, 0):
        probs = s_ref[:, r * CHUNK:(r + 1) * CHUNK]
        grad_probs = dot(grads, values_of(r), 1, 1)
        ds = (probs * (grad_probs - out_dot) * SCALE).astype(BF)
        dq = dq + dot(ds, keys_of(r), 1, 0)
        kt = dot(ds, queries, 0, 0).reshape(NZ, NY, SLOTS, HEAD)
        vt = dot(probs.astype(BF), grads, 0, 0).reshape(NZ, NY, SLOTS, HEAD)
        if r == 2:
            tb[0, :, :, :, 0:HEAD] = kt.astype(BF)
            tb[0, :, :, :, HEAD:KV] = vt.astype(BF)
            send(tb.at[0, :, 0], hl, es.at[0], er.at[0], to_right)
            send(tb.at[0, :, 1], hr, es.at[1], er.at[1], to_left)
            continue
        tf[:, :, :, 0:HEAD] = kt
        tf[:, :, :, HEAD:KV] = vt
        if r == 1:
            arrived(hl, er.at[0], to_left)
            tf[:, 0] = tf[:, 0] + hl[...].astype(F32)
            tb[1] = tf[...].astype(BF)
            send(tb.at[1], cl, es.at[2], er.at[2], to_right)
        elif r == 3:
            arrived(hr, er.at[1], to_right)
            tf[:, 1] = tf[:, 1] + hr[...].astype(F32)
            tb[2] = tf[...].astype(BF)
            send(tb.at[2], cr, es.at[3], er.at[3], to_left)
    for h in range(HEADS):
        dq_ref[:, h * HEAD:(h + 1) * HEAD] = dq[h * SLOTS:(h + 1) * SLOTS].astype(BF)
    arrived(cl, er.at[2], to_left)
    arrived(cr, er.at[3], to_right)
    tf[...] = tf[...] + cl[...].astype(F32) + cr[...].astype(F32)
    ub[...] = tf[...].astype(BF)
    for d in ZORDER:
        send(ub.at[(z + d) % NZ], zr.at[z], z_send.at[4, d], z_recv.at[4, d], zpeer(d))
    total = tf[z]
    for d in ARRIVE:
        zs = (z + NZ - d) % NZ
        arrived(zr.at[zs], z_recv.at[4, d], zpeer(d))
        total = total + zr[zs].astype(F32)
    vs[...] = total
    send(vs.at[1 - y], yr, z_send.at[4, 0], z_recv.at[4, 0], to_y)
    arrived(yr, z_recv.at[4, 0], to_y)
    gz[z] = (vs[y] + yr[...]).astype(BF)

    for d in ZORDER:
        send(gz.at[z], gz.at[z], z_send.at[5, d], z_recv.at[5, d], zpeer(d))
    for d in ARRIVE:
        zs = (z + NZ - d) % NZ
        arrived(gz.at[zs], z_recv.at[5, d], zpeer(d))
    slot_grads = gz[...].reshape(NZ * SLOTS, KV)

    fs, fr = x_send.at[2], x_recv.at[2]
    ts, tsr = x_send.at[3], x_recv.at[3]

    def weight_part(r):
        return dot(xz[chunk_of(r)].reshape(NZ * SLOTS, KV), slot_grads, 0, 0).reshape(
            NY, HEAD, KV
        )

    def row_part(xx):
        return dot(slot_grads, wg[xx].reshape(NY * HEAD, KV), 1, 1)

    for k in range(2):
        rsb[k] = row_part(2 * k + 1 - core).astype(BF)
    send(rsb, rsr, ts.at[0], tsr.at[0], to_sib)
    wb[0] = weight_part(2).astype(BF)
    send(wb.at[0, 0], whl, fs.at[0], fr.at[0], to_right)
    send(wb.at[0, 1], whr, fs.at[1], fr.at[1], to_left)
    for k in range(2):
        rf[k] = row_part(2 * k + core)
    arrived(rsr, tsr.at[0], to_sib)
    ryb[...] = (rf[1 - ylo] + rsr[1 - ylo].astype(F32)).astype(BF)
    send(ryb, ryr, ts.at[1], tsr.at[1], to_ylo)
    wf[...] = weight_part(1)
    arrived(whl, fr.at[0], to_left)
    wf[0] = wf[0] + whl[...].astype(F32)
    wb[1] = wf[...].astype(BF)
    send(wb.at[1], wcl, fs.at[2], fr.at[2], to_right)
    wf[...] = weight_part(3)
    arrived(whr, fr.at[1], to_right)
    wf[1] = wf[1] + whr[...].astype(F32)
    wb[2] = wf[...].astype(BF)
    send(wb.at[2], wcr, fs.at[3], fr.at[3], to_left)
    arrived(ryr, tsr.at[1], to_ylo)
    tz[...] = (
        (rf[ylo] + rsr[ylo].astype(F32) + ryr[...].astype(F32)).astype(BF).reshape(NZ, SLOTS, KV)
    )
    for d in ZORDER:
        send(tz.at[(z + d) % NZ], tr.at[z], z_send.at[6, d], z_recv.at[6, d], zpeer(d))
    tr[z] = tz[z]
    wf[...] = weight_part(0)
    arrived(wcl, fr.at[2], to_left)
    arrived(wcr, fr.at[3], to_right)
    wf[...] = wf[...] + wcl[...].astype(F32) + wcr[...].astype(F32)
    wyb[...] = wf[1 - y].astype(BF)
    send(wyb, wyr, fs.at[4], fr.at[4], to_y)

    for d in ARRIVE:
        zs = (z + NZ - d) % NZ
        arrived(tr.at[zs], z_recv.at[6, d], zpeer(d))
    for zs in range(NZ):
        rows = (tr[zs].astype(F32) * live).astype(BF)
        tg_ref[:, zs * KV:(zs + 1) * KV] = dot(hot, rows, 0, 0).astype(BF)

    arrived(wyr, fr.at[4], to_y)
    both = (wf[y] + wyr[...].astype(F32)).astype(BF)
    kwg_ref[...] = both[:, 0:HEAD]
    vwg_ref[...] = both[:, HEAD:KV]

    for cp in started:
        cp.wait_send()


def local(tokens, select_index, valid_count, queries, key_matrix, value_matrix, out_grad):
    vmem = pl.BlockSpec(memory_space=pltpu.VMEM)
    dma = pltpu.SemaphoreType.DMA
    V = pltpu.VMEM
    shape = jax.ShapeDtypeStruct
    scratch = [
        V((ROWS, MODEL // 2), BF),
        V((NZ, 2, SLOTS, KV), BF),
        V((NX, NZ, SLOTS, KV), BF),
        V((NX, NY, HEAD, KV), BF),
        V((NZ, SLOTS, KV), F32),
        V((NZ, SLOTS, KV), F32),
        V((NX * PER_X, SLOTS, KV), BF),
        V((QROWS, NX * CHUNK), F32),
        V((QROWS, HEAD), BF),
        V((QROWS, HEAD), BF),
        V((NZ, NY, SLOTS, KV), F32),
        V((3, NZ, NY, SLOTS, KV), BF),
        V((NZ, SLOTS, KV), BF),
        V((NZ, SLOTS, KV), BF),
        V((NZ, NY, SLOTS, KV), BF),
        V((NZ, NY, SLOTS, KV), BF),
        V((NZ, NY, SLOTS, KV), BF),
        V((NZ, NY, SLOTS, KV), BF),
        V((NY, SLOTS, KV), F32),
        V((SLOTS, KV), F32),
        V((NZ, SLOTS, KV), BF),
        V((3, NY, HEAD, KV), BF),
        V((NY, HEAD, KV), F32),
        V((HEAD, KV), BF),
        V((HEAD, KV), BF),
        V((NY, HEAD, KV), BF),
        V((NY, HEAD, KV), BF),
        V((HEAD, KV), BF),
        V((HEAD, KV), BF),
        V((2, NZ * SLOTS, KV), BF),
        V((2, NZ * SLOTS, KV), BF),
        V((2, NZ * SLOTS, KV), F32),
        V((NZ * SLOTS, KV), BF),
        V((NZ * SLOTS, KV), BF),
        V((NZ, SLOTS, KV), BF),
        V((NZ, SLOTS, KV), BF),
        dma, dma((7, NZ)), dma((7, NZ)), dma((4, 8)), dma((4, 8)), dma((4, NZ)), dma((4, NZ)),
    ]
    att, dq, tg, kwg, vwg = pl.pallas_call(
        kernel,
        out_shape=(
            shape((SLOTS, HEADS * HEAD), BF),
            shape((SLOTS, HEADS * HEAD), BF),
            shape((ROWS, MODEL // 4), BF),
            shape((HEAD, HEAD), BF),
            shape((HEAD, HEAD), BF),
        ),
        in_specs=[pl.BlockSpec(memory_space=pl.ANY)] + [vmem] * 6,
        out_specs=(vmem,) * 5,
        scratch_shapes=scratch,
        compiler_params=pltpu.CompilerParams(
            collective_id=0, has_side_effects=True, vmem_limit_bytes=60 * 1024 * 1024
        ),
    )(
        tokens, select_index.reshape(1, -1), valid_count.reshape(1, -1), queries,
        key_matrix, value_matrix, out_grad,
    )
    return att, dq, tg, kwg, vwg


def solution(mesh):
    in_specs = (
        P("ctx", None), P("ctx"), P(), P("ctx", "tp"), P("ctx", "tp"), P("ctx", "tp"),
        P("ctx", "tp"),
    )
    out_specs = (P("ctx", "tp"),) * 5
    return jax.shard_map(local, mesh=mesh, in_specs=in_specs, out_specs=out_specs, check_vma=False)
```

time: 1210 us -> 103 us (0.09)
  waiting for transfers between devices: 1130 us -> 0 us
  Pallas kernels: 0 us -> 92 us
  matrix products: 19.4 us -> 0 us
  local copies, waits for them, and re-layouts: 24.3 us -> 8 us
  between operations: 14.3 us -> 0.64 us
    reduce_scatter x3 -> x0, waiting for transfers between devices: 787 us -> none  [the longest x1 392 us: local(): lax.psum_scatter(kv_terms, 'ctx', scatter_dimension=0, tiled=True)]
    all_gather x3 -> x0, waiting for transfers between devices: 342 us -> none  [the longest x1 116 us: local(): lax.all_gather(key_matrix, 'ctx', axis=0, tiled=True)]
    pallas_call x0 -> x1, Pallas kernels: none -> 92 us  [local(): pl.pallas_call(kernel, out_shape=(shape((SLOTS, HEADS * HEAD), BF), shape...]
    dot_general x10 -> x0, matrix products: 19.4 us -> none  [the longest x1 4.62 us: local(): lax.dot_general(picked, own_grads, (((0,), (0,)), ((), ())), preferred_el...]
  transfers between devices with their start and end apart: 6 -> 0, of which waited for: 6 -> 0; matrix products, arithmetic and copies ran while one was open for 2% -> 0% of each run, Pallas kernels for 0% -> 0%
where the time goes in v1:
time: 103 us; the launch traced here: 101 us
  Pallas kernels  92 us (89%)
  local copies, waits for them, and re-layouts  8 us (8%)
    pallas_call x1, Pallas kernels, local(): pl.pallas_call(kernel, out_shape=(shape((SLOTS, HEADS * HEAD), BF), shape...  92 us
    unnamed x5, local copies, waits for them, and re-layouts  8 us

profile of v1, /device:TPU:8, one launch (start us, length us, event | category | flops | bytes accessed | tf_op | source)
XLA Modules:
  0.0 100.6 jit_solution(5827999361302889566)
XLA Ops:
  0.6 92.0 %shard_map.110 = (bf16[32,1024]{1,0:T(8,128)(2,1)}, bf16[32,1024]{1,0:T(8,128)(2,1)}, bf16[256,2048]{1,0:T(8,128)(2,1)}, bf16[128,128]{1,0:T(8,128)(2,1)}, bf16[128,128]{1,0:T(8,128)(2,1)}) custom-call(bf16[256,8192]{1,0:T(8,128)(2,1)} %tok_hbm.1, s32[1,32]{1,0:T(1,128)} %bitcast.2, s32[1,64]{1,0:T(1,128)} %bitcast.3, bf16[32,1024]{1,0:T(8,128)(2,1)} %q_ref.1, ...), custom_call_target="tpu_custom_call" | custom-call | tf_op jit(solution)/shard_map/pallas_call | solution.py:410
  92.6 1.5 %copy.17 = bf16[32,1024]{1,0:T(8,128)(2,1)} copy(bf16[32,1024]{1,0:T(8,128)(2,1)} %get-tuple-element.10) | data formatting | bytes 131072
  94.1 1.5 %copy.18 = bf16[32,1024]{1,0:T(8,128)(2,1)} copy(bf16[32,1024]{1,0:T(8,128)(2,1)} %get-tuple-element.11) | data formatting | bytes 131072
  95.6 2.3 %copy.19 = bf16[256,2048]{1,0:T(8,128)(2,1)} copy(bf16[256,2048]{1,0:T(8,128)(2,1)} %get-tuple-element.12) | data formatting | bytes 2097152
  97.9 1.4 %copy.20 = bf16[128,128]{1,0:T(8,128)(2,1)} copy(bf16[128,128]{1,0:T(8,128)(2,1)} %get-tuple-element.13) | data formatting | bytes 65536
  99.2 1.4 %copy.21 = bf16[128,128]{1,0:T(8,128)(2,1)} copy(bf16[128,128]{1,0:T(8,128)(2,1)} %get-tuple-element.14) | data formatting | bytes 65536

commit v2 on v1

v2 whole, which is shorter than its diff:
```python
import math

import jax
import jax.numpy as jnp
from jax import lax
from jax.experimental import pallas as pl
from jax.experimental.pallas import tpu as pltpu
from jax.sharding import PartitionSpec as P

NX, NZ, NY = 4, 8, 2
HEAD = 128
SLOTS = 32
KV = 2 * HEAD
HEADS = 8
ROWS = 256
MODEL = 8192
PER_X = NZ * NY
CHUNK = PER_X * SLOTS
QROWS = HEADS * SLOTS
SCALE = 1.0 / math.sqrt(HEAD)
NEG = -1e30
BF = jnp.bfloat16
F32 = jnp.float32
ZORDER = (4, 3, 5, 2, 6, 1, 7)
ARRIVE = (1, 7, 2, 6, 3, 5, 4)
NEAREST = (0,) + ARRIVE
FARTHEST = ZORDER + (0,)
XORDER = ((2, 1), (2, 0), (1, 1), (3, 1), (1, 0), (3, 0), (0, 1))


def dot(a, b, ca, cb):
    return lax.dot_general(a, b, (((ca,), (cb,)), ((), ())), preferred_element_type=F32)


def kernel(
    tok_hbm, sel_hbm, vc_hbm, q_hbm, wk_hbm, wv_hbm, g_hbm,
    att_ref, dq_ref, rows_ref, wgr_ref,
    tok, sel_ref, vc_ref, q_ref, g_ref, pz, xz, wg, pf, pk, pv, rk, rv, kv, s_ref, qs, gs,
    tf, tf2, tb, hy, fb, fx, nl, nr, ub, zr, gz,
    wb, wf, wx, rsb, rsr, rf, ryb, ryr, tz, tr,
    in_sem, w_send, w_recv, z_send, z_recv, x_send, x_recv, ag_send, ag_recv, rs_send, rs_recv,
    t_send, t_recv,
):
    c = lax.axis_index("ctx")
    t = lax.axis_index("tp")
    x = c // PER_X
    z = (c // NY) % NZ
    y = c % NY
    core = t % 2
    ylo = t // 2
    right = (x + 1) % NX
    left = (x + NX - 1) % NX
    far = (x + 2) % NX

    def at(xx, zz, yy):
        return {"ctx": (xx * NZ + zz) * NY + yy, "tp": t}

    def zpeer(d):
        return at(x, (z + d) % NZ, y)

    def zpeer_y(d):
        return at(x, (z + d) % NZ, 1 - y)

    def half_of(k):
        return y if k == 0 else 1 - y

    def xpeer(r, k):
        return at((x + r) % NX, z, half_of(k))

    to_right = at(right, z, y)
    to_left = at(left, z, y)
    to_far = at(far, z, y)
    to_y = at(x, z, 1 - y)
    to_sib = {"ctx": c, "tp": 2 * ylo + 1 - core}
    to_ylo = {"ctx": c, "tp": 2 * (1 - ylo) + core}

    started = []

    def copy(src, dst, ssem, rsem, dev):
        return pltpu.make_async_remote_copy(
            src_ref=src, dst_ref=dst, send_sem=ssem, recv_sem=rsem,
            device_id=dev, device_id_type=pl.DeviceIdType.MESH,
        )

    def send(src, dst, ssem, rsem, dev):
        cp = copy(src, dst, ssem, rsem, dev)
        cp.start()
        started.append(cp)

    def arrived(dst, rsem, dev):
        copy(dst, dst, rsem, rsem, dev).wait_recv()

    barrier = pltpu.get_barrier_semaphore()
    partners = [zpeer(d) for d in range(1, NZ)] + [zpeer_y(d) for d in range(1, NZ)]
    partners += [xpeer(r, k) for r in range(1, NX) for k in range(2)] + [to_y, to_sib, to_ylo]
    for dev in partners:
        pl.semaphore_signal(barrier, inc=1, device_id=dev, device_id_type=pl.DeviceIdType.MESH)

    x_cols = NZ * KV
    loads = [pltpu.make_async_copy(sel_hbm, sel_ref, in_sem.at[0])]
    for k in range(2):
        c0 = pl.multiple_of((2 * core + k) * x_cols, x_cols)
        loads.append(
            pltpu.make_async_copy(tok_hbm.at[:, pl.ds(c0, x_cols)], tok.at[k], in_sem.at[1 + k])
        )
    loads.append(pltpu.make_async_copy(wk_hbm, wg.at[x, y, :, pl.ds(0, HEAD)], in_sem.at[3]))
    loads.append(pltpu.make_async_copy(wv_hbm, wg.at[x, y, :, pl.ds(HEAD, HEAD)], in_sem.at[4]))
    loads.append(pltpu.make_async_copy(vc_hbm, vc_ref, in_sem.at[5]))
    loads.append(pltpu.make_async_copy(q_hbm, q_ref, in_sem.at[6]))
    loads.append(pltpu.make_async_copy(g_hbm, g_ref, in_sem.at[7]))
    for cp in loads:
        cp.start()

    loads[0].wait()
    sel_row = jnp.broadcast_to(sel_ref[...], (SLOTS, SLOTS))
    i0 = lax.broadcasted_iota(jnp.int32, (SLOTS, SLOTS), 0)
    i1 = lax.broadcasted_iota(jnp.int32, (SLOTS, SLOTS), 1)
    sel_col = jnp.sum(jnp.where(i0 == i1, sel_row, 0), axis=1, keepdims=True)
    hot = jnp.where(
        lax.broadcasted_iota(jnp.int32, (SLOTS, ROWS), 1) == sel_col, 1.0, 0.0
    ).astype(BF)
    for k in range(2):
        loads[1 + k].wait()
        for zt in range(NZ):
            pz[zt, k] = dot(hot, tok[k, :, zt * KV:(zt + 1) * KV], 1, 0).astype(BF)
    xz[pl.ds(2 * core, 2), z] = pz[z]
    loads[3].wait()
    loads[4].wait()

    pl.semaphore_wait(barrier, len(partners))

    mine = wg.at[x, y]
    for r, k in XORDER:
        send(mine, mine, w_send.at[r, k], w_recv.at[r, k], xpeer(r, k))
    for d in ZORDER:
        send(
            pz.at[(z + d) % NZ], xz.at[pl.ds(2 * core, 2), z],
            z_send.at[0, d], z_recv.at[0, d], zpeer(d),
        )
    send(pz.at[z], xz.at[pl.ds(2 * core, 2), z], z_send.at[1, 0], z_recv.at[1, 0], to_sib)

    for cp in loads[5:]:
        cp.wait()
    vc = vc_ref[...]
    own_count = jnp.sum(
        jnp.where(lax.broadcasted_iota(jnp.int32, vc.shape, 1) == c, vc, 0), axis=1, keepdims=True
    )
    live_col = lax.broadcasted_iota(jnp.int32, (SLOTS, 1), 0) < own_count
    live = jnp.where(live_col, 1.0, 0.0)
    qpos = jnp.where(live_col, sel_col, ROWS).astype(F32)
    qpos_all = jnp.concatenate([qpos] * HEADS, axis=0)
    for h in range(HEADS):
        qs[h * SLOTS:(h + 1) * SLOTS, :] = q_ref[:, h * HEAD:(h + 1) * HEAD]
        gs[h * SLOTS:(h + 1) * SLOTS, :] = (
            g_ref[:, h * HEAD:(h + 1) * HEAD].astype(F32) * live
        ).astype(BF)

    def relay_picked(d):
        zs = (z + NZ - d) % NZ
        block = xz.at[pl.ds(2 * core, 2), zs]
        arrived(block, z_recv.at[0, d], zpeer(d))
        send(block, block, z_send.at[1, d], z_recv.at[1, d], to_sib)

    for d in ARRIVE:
        relay_picked(d)
    for r, k in XORDER:
        arrived(wg.at[(x + NX - r) % NX, half_of(k)], w_recv.at[r, k], xpeer(r, k))
    for d in NEAREST:
        zs = (z + NZ - d) % NZ
        arrived(xz.at[pl.ds(2 * (1 - core), 2), zs], z_recv.at[1, d], to_sib)

    acc = jnp.zeros((NZ * SLOTS, KV), F32)
    for xx in range(NX):
        acc = acc + dot(
            xz[xx].reshape(NZ * SLOTS, KV), wg[xx].reshape(NY * HEAD, KV), 1, 0
        )
    pf[...] = acc.reshape(NZ, SLOTS, KV)
    pk[...] = pf[:, :, 0:HEAD]
    pv[...] = pf[:, :, HEAD:KV].astype(BF)
    for d in ZORDER:
        zt = (z + d) % NZ
        send(pk.at[zt], rk.at[z], z_send.at[2, d], z_recv.at[2, d], zpeer(d))
        send(pv.at[zt], rv.at[z], t_send.at[4, d], t_recv.at[4, d], zpeer(d))
    key_sum = pf[z, :, 0:HEAD]
    value_sum = pf[z, :, HEAD:KV]
    for d in ARRIVE:
        zs = (z + NZ - d) % NZ
        arrived(rk.at[zs], z_recv.at[2, d], zpeer(d))
        key_sum = key_sum + rk[zs]
        arrived(rv.at[zs], t_recv.at[4, d], zpeer(d))
        value_sum = value_sum + rv[zs].astype(F32)
    kv[c, :, 0:HEAD] = key_sum.astype(BF)
    kv[c, :, HEAD:KV] = value_sum.astype(BF)

    def one(xx, zz, yy):
        return kv.at[(xx * NZ + zz) * NY + yy]

    def spread_near(block, d, k):
        send(block, block, ag_send.at[k, d], ag_recv.at[k, d], to_right)
        send(block, block, ag_send.at[k + 1, d], ag_recv.at[k + 1, d], to_left)

    def own_block(d):
        block = one(x, (z + NZ - d) % NZ, y)
        if d:
            arrived(block, z_recv.at[3, d], zpeer(d))
        send(block, block, ag_send.at[4, d], ag_recv.at[4, d], to_far)
        spread_near(block, d, 0)

    def peer_block(d):
        block = one(x, (z + NZ - d) % NZ, 1 - y)
        arrived(block, z_recv.at[6, d], zpeer_y(d))
        spread_near(block, d, 2)

    def far_block(d):
        block = one(far, (z + NZ - d) % NZ, y)
        arrived(block, ag_recv.at[4, d], to_far)
        send(block, block, ag_send.at[5, d], ag_recv.at[5, d], to_y)

    own = one(x, z, y)
    for d in ZORDER:
        send(own, own, z_send.at[3, d], z_recv.at[3, d], zpeer(d))
    own_block(0)
    for d in FARTHEST:
        send(own, own, z_send.at[6, d], z_recv.at[6, d], zpeer_y(d))
    for d in ARRIVE:
        own_block(d)
    peer_block(0)
    far_block(0)
    for d in ARRIVE:
        peer_block(d)
        far_block(d)
    for d in NEAREST:
        zs = (z + NZ - d) % NZ
        arrived(one(left, zs, y), ag_recv.at[0, d], to_left)
        arrived(one(right, zs, y), ag_recv.at[1, d], to_right)
        arrived(one(left, zs, 1 - y), ag_recv.at[2, d], to_left)
        arrived(one(right, zs, 1 - y), ag_recv.at[3, d], to_right)
    for d in NEAREST:
        arrived(one(far, (z + NZ - d) % NZ, 1 - y), ag_recv.at[5, d], to_y)

    vc8 = jnp.broadcast_to(vc.astype(F32), (8, NX * PER_X)).astype(BF)
    sel8 = jnp.broadcast_to(sel_ref[...].astype(F32), (8, SLOTS)).astype(BF)
    jslot = lax.broadcasted_iota(jnp.int32, (SLOTS, CHUNK), 1) % SLOTS
    spread = jnp.where(jslot == lax.broadcasted_iota(jnp.int32, (SLOTS, CHUNK), 0), 1.0, 0.0)
    sel_keys = dot(sel8, spread.astype(BF), 1, 0)[0:1]
    queries = qs[...]
    grads = gs[...]

    def chunk_of(r):
        return (x + r) % NX

    def keys_of(r):
        return kv[pl.ds(chunk_of(r) * PER_X, PER_X), :, 0:HEAD].reshape(CHUNK, HEAD)

    def values_of(r):
        return kv[pl.ds(chunk_of(r) * PER_X, PER_X), :, HEAD:KV].reshape(CHUNK, HEAD)

    top = jnp.full((QROWS, 1), NEG, F32)
    for r in range(NX):
        shard = chunk_of(r) * PER_X + lax.broadcasted_iota(
            jnp.int32, (NX * PER_X, CHUNK), 1
        ) // SLOTS
        expand = jnp.where(
            shard == lax.broadcasted_iota(jnp.int32, (NX * PER_X, CHUNK), 0), 1.0, 0.0
        )
        counts = dot(vc8, expand.astype(BF), 1, 0)[0:1]
        shard_row = chunk_of(r) * PER_X + lax.broadcasted_iota(jnp.int32, (1, CHUNK), 1) // SLOTS
        slot_row = (lax.broadcasted_iota(jnp.int32, (1, CHUNK), 1) % SLOTS).astype(F32)
        place = jnp.where(shard_row < c, -1.0, jnp.where(shard_row > c, 1e6, sel_keys))
        place = jnp.where(slot_row < counts, place, 1e6)
        scores = dot(queries, keys_of(r), 1, 1) * SCALE
        scores = jnp.where(place <= qpos_all, scores, NEG)
        s_ref[:, r * CHUNK:(r + 1) * CHUNK] = scores
        top = jnp.maximum(top, jnp.max(scores, axis=1, keepdims=True))
    norm = jnp.zeros((QROWS, 1), F32)
    for r in range(NX):
        terms = jnp.exp(s_ref[:, r * CHUNK:(r + 1) * CHUNK] - top)
        s_ref[:, r * CHUNK:(r + 1) * CHUNK] = terms
        norm = norm + jnp.sum(terms, axis=1, keepdims=True)
    inv = 1.0 / norm
    out = jnp.zeros((QROWS, HEAD), F32)
    for r in range(NX):
        probs = s_ref[:, r * CHUNK:(r + 1) * CHUNK] * inv
        s_ref[:, r * CHUNK:(r + 1) * CHUNK] = probs
        out = out + dot(probs.astype(BF), values_of(r), 1, 0)
    live_all = jnp.concatenate([live] * HEADS, axis=0)
    attended = (out * live_all).astype(BF)
    for h in range(HEADS):
        att_ref[:, h * HEAD:(h + 1) * HEAD] = attended[h * SLOTS:(h + 1) * SLOTS]
    out_dot = jnp.sum(grads.astype(F32) * attended.astype(F32), axis=1, keepdims=True)

    dq = jnp.zeros((QROWS, HEAD), F32)

    def column(r, dq):
        probs = s_ref[:, r * CHUNK:(r + 1) * CHUNK]
        grad_probs = dot(grads, values_of(r), 1, 1)
        ds = (probs * (grad_probs - out_dot) * SCALE).astype(BF)
        dq = dq + dot(ds, keys_of(r), 1, 0)
        kt = dot(ds, queries, 0, 0).reshape(NZ, NY, SLOTS, HEAD)
        vt = dot(probs.astype(BF), grads, 0, 0).reshape(NZ, NY, SLOTS, HEAD)
        return dq, kt, vt

    dq, kt, vt = column(2, dq)
    tf2[:, :, :, 0:HEAD] = kt
    tf2[:, :, :, HEAD:KV] = vt
    tb[0] = tf2[...].astype(BF)
    for d in FARTHEST:
        zt = (z + d) % NZ
        send(tb.at[0, zt, 1 - y], hy.at[zt], rs_send.at[0, d], rs_recv.at[0, d], to_y)
    for k, r in ((1, 1), (2, 3)):
        dq, kt, vt = column(r, dq)
        tb[k, :, :, :, 0:HEAD] = kt.astype(BF)
        tb[k, :, :, :, HEAD:KV] = vt.astype(BF)

    def near(d):
        zt = (z + d) % NZ
        send(tb.at[1, zt], nl.at[zt], rs_send.at[1, d], rs_recv.at[1, d], to_right)
        send(tb.at[2, zt], nr.at[zt], rs_send.at[2, d], rs_recv.at[2, d], to_left)

    def distant(d):
        zt = (z + d) % NZ
        arrived(hy.at[zt], rs_recv.at[0, d], to_y)
        fb[zt] = (tf2[zt, y] + hy[zt].astype(F32)).astype(BF)
        send(fb.at[zt], fx.at[zt], rs_send.at[3, d], rs_recv.at[3, d], to_far)

    for d in FARTHEST[:3]:
        near(d)
    dq, kt, vt = column(0, dq)
    tf[:, :, :, 0:HEAD] = kt
    tf[:, :, :, HEAD:KV] = vt
    for d in FARTHEST[:3]:
        distant(d)
    for d in FARTHEST[3:]:
        near(d)
        distant(d)
    for h in range(HEADS):
        dq_ref[:, h * HEAD:(h + 1) * HEAD] = dq[h * SLOTS:(h + 1) * SLOTS].astype(BF)
    for d in FARTHEST:
        zt = (z + d) % NZ
        arrived(nl.at[zt], rs_recv.at[1, d], to_left)
        arrived(nr.at[zt], rs_recv.at[2, d], to_right)
        tf[zt] = tf[zt] + nl[zt].astype(F32) + nr[zt].astype(F32)
        arrived(fx.at[zt], rs_recv.at[3, d], to_far)
        tf[zt, y] = tf[zt, y] + fx[zt].astype(F32)
        ub[zt] = tf[zt].astype(BF)
        if d:
            send(ub.at[zt, y], zr.at[z, y], z_send.at[4, d], z_recv.at[4, d], zpeer(d))
        send(ub.at[zt, 1 - y], zr.at[z, y], t_send.at[0, d], t_recv.at[0, d], zpeer_y(d))
    total = tf[z, y]
    arrived(zr.at[z, 1 - y], t_recv.at[0, 0], to_y)
    total = total + zr[z, 1 - y].astype(F32)
    for d in ARRIVE:
        zs = (z + NZ - d) % NZ
        arrived(zr.at[zs, y], z_recv.at[4, d], zpeer(d))
        arrived(zr.at[zs, 1 - y], t_recv.at[0, d], zpeer_y(d))
        total = total + zr[zs, y].astype(F32) + zr[zs, 1 - y].astype(F32)
    gz[z] = total.astype(BF)

    for d in ZORDER:
        send(gz.at[z], gz.at[z], z_send.at[5, d], z_recv.at[5, d], zpeer(d))
    for d in ARRIVE:
        zs = (z + NZ - d) % NZ
        arrived(gz.at[zs], z_recv.at[5, d], zpeer(d))
    slot_grads = gz[...].reshape(NZ * SLOTS, KV)


    def weight_part(r):
        return dot(xz[chunk_of(r)].reshape(NZ * SLOTS, KV), slot_grads, 0, 0).reshape(
            NY, HEAD, KV
        )

    def row_part(xx):
        return dot(slot_grads, wg[xx].reshape(NY * HEAD, KV), 1, 1).reshape(NZ, SLOTS, KV)

    for k in range(2):
        rsb[:, k] = row_part(2 * k + 1 - core).astype(BF)
    for d in FARTHEST:
        zt = (z + d) % NZ
        send(rsb.at[zt], rsr.at[zt], t_send.at[1, d], t_recv.at[1, d], to_sib)
    for r in (2, 1, 3):
        wb[r] = weight_part(r).astype(BF)
        for k in (1, 0):
            send(wb.at[r, half_of(k)], wx.at[r, k], x_send.at[r, k], x_recv.at[r, k], xpeer(r, k))
    for k in range(2):
        rf[:, k] = row_part(2 * k + core)
    for d in FARTHEST:
        zt = (z + d) % NZ
        arrived(rsr.at[zt], t_recv.at[1, d], to_sib)
        ryb[zt] = (rf[zt, 1 - ylo] + rsr[zt, 1 - ylo].astype(F32)).astype(BF)
        send(ryb.at[zt], ryr.at[zt], t_send.at[2, d], t_recv.at[2, d], to_ylo)
    wf[...] = weight_part(0)
    wb[0] = wf[...].astype(BF)
    send(wb.at[0, 1 - y], wx.at[0, 1], x_send.at[0, 1], x_recv.at[0, 1], to_y)
    for d in FARTHEST:
        zt = (z + d) % NZ
        arrived(ryr.at[zt], t_recv.at[2, d], to_ylo)
        tz[zt] = (
            rf[zt, ylo] + rsr[zt, ylo].astype(F32) + ryr[zt].astype(F32)
        ).astype(BF)
        if d:
            send(tz.at[zt], tr.at[z], t_send.at[3, d], t_recv.at[3, d], zpeer(d))
    tr[z] = tz[z]
    for d in ARRIVE:
        zs = (z + NZ - d) % NZ
        arrived(tr.at[zs], t_recv.at[3, d], zpeer(d))
    for zs in range(NZ):
        rows_ref[:, zs * KV:(zs + 1) * KV] = (tr[zs].astype(F32) * live).astype(BF)

    total = wf[y]
    for r, k in XORDER:
        arrived(wx.at[r, k], x_recv.at[r, k], xpeer(NX - r, k))
        total = total + wx[r, k].astype(F32)
    wgr_ref[...] = total.astype(BF)

    for cp in started:
        cp.wait_send()


def finish(
    sel_ref, att_in, dq_in, rows_ref, wgr_ref, att_ref, dq_ref, tg_ref, kwg_ref, vwg_ref
):
    sel_row = jnp.broadcast_to(sel_ref[...], (ROWS, SLOTS))
    place = jnp.where(
        lax.broadcasted_iota(jnp.int32, (ROWS, SLOTS), 0) == sel_row, 1.0, 0.0
    ).astype(BF)
    for k in range(NZ):
        tg_ref[:, k * KV:(k + 1) * KV] = dot(
            place, rows_ref[:, k * KV:(k + 1) * KV], 1, 0
        ).astype(BF)
    att_ref[...] = att_in[...]
    dq_ref[...] = dq_in[...]
    kwg_ref[...] = wgr_ref[:, 0:HEAD]
    vwg_ref[...] = wgr_ref[:, HEAD:KV]


def local(tokens, select_index, valid_count, queries, key_matrix, value_matrix, out_grad):
    vmem = pl.BlockSpec(memory_space=pltpu.VMEM)
    dma = pltpu.SemaphoreType.DMA
    V = pltpu.VMEM
    shape = jax.ShapeDtypeStruct
    block = (NZ, SLOTS, KV)
    pairs = (NZ, NY, SLOTS, KV)
    scratch = [
        V((2, ROWS, NZ * KV), BF),
        V((1, SLOTS), jnp.int32),
        V((1, NX * PER_X), jnp.int32),
        V((SLOTS, HEADS * HEAD), BF),
        V((SLOTS, HEADS * HEAD), BF),
        V((NZ, 2, SLOTS, KV), BF),
        V((NX, NZ, SLOTS, KV), BF),
        V((NX, NY, HEAD, KV), BF),
        V(block, F32),
        V((NZ, SLOTS, HEAD), F32),
        V((NZ, SLOTS, HEAD), BF),
        V((NZ, SLOTS, HEAD), F32),
        V((NZ, SLOTS, HEAD), BF),
        V((NX * PER_X, SLOTS, KV), BF),
        V((QROWS, NX * CHUNK), F32),
        V((QROWS, HEAD), BF),
        V((QROWS, HEAD), BF),
        V(pairs, F32),
        V(pairs, F32),
        V((3,) + pairs, BF),
        V(block, BF),
        V(block, BF),
        V(block, BF),
        V(pairs, BF),
        V(pairs, BF),
        V(pairs, BF),
        V(pairs, BF),
        V(block, BF),
        V((NX, NY, HEAD, KV), BF),
        V((NY, HEAD, KV), F32),
        V((NX, 2, HEAD, KV), BF),
        V((NZ, 2, SLOTS, KV), BF),
        V((NZ, 2, SLOTS, KV), BF),
        V((NZ, 2, SLOTS, KV), F32),
        V(block, BF),
        V(block, BF),
        V(block, BF),
        V(block, BF),
        dma((8,)), dma((NX, 2)), dma((NX, 2)), dma((7, NZ)), dma((7, NZ)), dma((NX, 2)),
        dma((NX, 2)),
        dma((6, NZ)), dma((6, NZ)), dma((4, NZ)), dma((4, NZ)), dma((5, NZ)), dma((5, NZ)),
    ]
    sel = select_index.reshape(1, -1)
    att, dq, rows, wgr = pl.pallas_call(
        kernel,
        out_shape=(
            shape((SLOTS, HEADS * HEAD), BF),
            shape((SLOTS, HEADS * HEAD), BF),
            shape((SLOTS, MODEL // 4), BF),
            shape((HEAD, KV), BF),
        ),
        in_specs=[pl.BlockSpec(memory_space=pl.ANY)] * 7,
        out_specs=(vmem,) * 4,
        scratch_shapes=scratch,
        compiler_params=pltpu.CompilerParams(
            collective_id=0, has_side_effects=True, vmem_limit_bytes=62 * 1024 * 1024
        ),
    )(tokens, sel, valid_count.reshape(1, -1), queries, key_matrix, value_matrix, out_grad)
    return pl.pallas_call(
        finish,
        out_shape=(
            shape((SLOTS, HEADS * HEAD), BF),
            shape((SLOTS, HEADS * HEAD), BF),
            shape((ROWS, MODEL // 4), BF),
            shape((HEAD, HEAD), BF),
            shape((HEAD, HEAD), BF),
        ),
        in_specs=[vmem] * 5,
        out_specs=(vmem,) * 5,
        compiler_params=pltpu.CompilerParams(vmem_limit_bytes=6 * 1024 * 1024),
    )(sel, att, dq, rows, wgr)


def solution(mesh):
    in_specs = (
        P("ctx", None), P("ctx"), P(), P("ctx", "tp"), P("ctx", "tp"), P("ctx", "tp"),
        P("ctx", "tp"),
    )
    out_specs = (P("ctx", "tp"),) * 5
    return jax.shard_map(local, mesh=mesh, in_specs=in_specs, out_specs=out_specs, check_vma=False)
```

time: 103 us -> 87.1 us (0.85); the launches traced: 101 us -> 86.8 us
  Pallas kernels: 92 us -> 82.7 us
  local copies, waits for them, and re-layouts: 8 us -> 3.42 us
    pallas_call x1, Pallas kernels: 92 us -> 81.4 us  [local(): pl.pallas_call(kernel, out_shape=(shape((SLOTS, HEADS * HEAD), BF), shape...]
    unnamed x5 -> x10, local copies, waits for them, and re-layouts: 8 us -> 3.42 us
    pallas_call x0 -> x1, Pallas kernels: none -> 1.38 us  [local(): pl.pallas_call(finish, out_shape=(shape((SLOTS, HEADS * HEAD), BF), shape...]
where the time goes in v2:
time: 87.1 us; the launch traced here: 86.8 us
  Pallas kernels  82.7 us (95%)
  local copies, waits for them, and re-layouts  3.42 us (4%)
    pallas_call x1, Pallas kernels, local(): pl.pallas_call(kernel, out_shape=(shape((SLOTS, HEADS * HEAD), BF), shape...  81.4 us
    unnamed x10, local copies, waits for them, and re-layouts  3.42 us

profile of v2, /device:TPU:8, one launch (start us, length us, event | category | flops | bytes accessed | tf_op | source)
XLA Modules:
  0.0 86.8 jit_solution(3625906913891151990)
XLA Ops:
  0.6 0.0 copy-start.4
  0.6 81.4 %shard_map.110 = (bf16[32,1024]{1,0:T(8,128)(2,1)}, bf16[32,1024]{1,0:T(8,128)(2,1)}, bf16[32,2048]{1,0:T(8,128)(2,1)}, bf16[128,256]{1,0:T(8,128)(2,1)}) custom-call(bf16[256,8192]{1,0:T(8,128)(2,1)} %tok_hbm.1, s32[1,32]{1,0:T(1,128)} %bitcast.2, s32[1,64]{1,0:T(1,128)} %bitcast.4, bf16[32,1024]{1,0:T(8,128)(2,1)} %q_hbm.1, bf16[128,128]{1,0:T(8,128)(2,1)} %wk_hbm.1, ...), custom_call_target="tpu_custom_call" | custom-call | tf_op jit(solution)/shard_map/pallas_call | solution.py:487
  82.0 0.0 copy-done.4
  82.0 0.0 copy-start
  82.0 0.9 %copy-done = bf16[32,2048]{1,0:T(8,128)(2,1)S(1)} copy-done((bf16[32,2048]{1,0:T(8,128)(2,1)S(1)}, bf16[32,2048]{1,0:T(8,128)(2,1)}, u32[]{:S(2)}) %copy-start) | copy-done | bytes 131096
  82.9 0.0 copy-start.1
  82.9 0.8 copy-done.1
  83.8 0.0 copy-start.2
  83.8 0.8 copy-done.2
  84.6 0.0 copy-start.3
  84.6 0.8 copy-done.3
  85.4 1.4 %shard_map.111 = (bf16[32,1024]{1,0:T(8,128)(2,1)}, bf16[32,1024]{1,0:T(8,128)(2,1)}, bf16[256,2048]{1,0:T(8,128)(2,1)}, bf16[128,128]{1,0:T(8,128)(2,1)}, bf16[128,128]{1,0:T(8,128)(2,1)}) custom-call(s32[1,32]{1,0:T(1,128)S(1)} %bitcast.3, bf16[32,1024]{1,0:T(8,128)(2,1)S(1)} %copy-done.1, bf16[32,1024]{1,0:T(8,128)(2,1)S(1)} %copy-done.2, ...), custom_call_target="tpu_custom_call" | custom-call | tf_op jit(solution)/shard_map/pallas_call | solution.py:502
Async XLA Ops:
  0.6 81.4 %copy-start.4 = (s32[32]{0:T(128)S(1)}, s32[32]{0:T(128)}, u32[]{:S(2)}) copy-start(s32[32]{0:T(128)} %param.8) | copy-start | bytes 388
  82.0 0.9 %copy-start = (bf16[32,2048]{1,0:T(8,128)(2,1)S(1)}, bf16[32,2048]{1,0:T(8,128)(2,1)}, u32[]{:S(2)}) copy-start(bf16[32,2048]{1,0:T(8,128)(2,1)} %get-tuple-element.11.rows_ref) | copy-start | bytes 393220
  82.9 0.8 copy-start.1
  83.8 0.8 copy-start.2
  84.6 0.8 copy-start.3

commit v3 on v2

--- a/solution.py
+++ b/solution.py
@@ -203,6 +203,8 @@
         block = one(x, (z + NZ - d) % NZ, y)
         if d:
             arrived(block, z_recv.at[3, d], zpeer(d))
+        if d == 4:
+            send(block, block, ag_send.at[5, d], ag_recv.at[5, d], xpeer(2, 1))
         send(block, block, ag_send.at[4, d], ag_recv.at[4, d], to_far)
         spread_near(block, d, 0)
 
@@ -214,29 +216,39 @@
     def far_block(d):
         block = one(far, (z + NZ - d) % NZ, y)
         arrived(block, ag_recv.at[4, d], to_far)
-        send(block, block, ag_send.at[5, d], ag_recv.at[5, d], to_y)
+        if d != 4:
+            send(block, block, ag_send.at[5, d], ag_recv.at[5, d], to_y)
 
     own = one(x, z, y)
-    for d in ZORDER:
+    send(own, own, z_send.at[6, 0], z_recv.at[6, 0], to_y)
+    for d in ARRIVE:
         send(own, own, z_send.at[3, d], z_recv.at[3, d], zpeer(d))
     own_block(0)
-    for d in FARTHEST:
+    for d in ARRIVE:
         send(own, own, z_send.at[6, d], z_recv.at[6, d], zpeer_y(d))
-    for d in ARRIVE:
-        own_block(d)
+    own_block(1)
+    own_block(7)
     peer_block(0)
+    own_block(2)
+    own_block(6)
     far_block(0)
-    for d in ARRIVE:
-        peer_block(d)
-        far_block(d)
-    for d in NEAREST:
-        zs = (z + NZ - d) % NZ
-        arrived(one(left, zs, y), ag_recv.at[0, d], to_left)
-        arrived(one(right, zs, y), ag_recv.at[1, d], to_right)
-        arrived(one(left, zs, 1 - y), ag_recv.at[2, d], to_left)
-        arrived(one(right, zs, 1 - y), ag_recv.at[3, d], to_right)
-    for d in NEAREST:
-        arrived(one(far, (z + NZ - d) % NZ, 1 - y), ag_recv.at[5, d], to_y)
+    own_block(3)
+    own_block(5)
+    peer_block(1)
+    peer_block(7)
+    own_block(4)
+    far_block(1)
+    far_block(7)
+    peer_block(2)
+    peer_block(6)
+    far_block(2)
+    far_block(6)
+    peer_block(3)
+    peer_block(5)
+    far_block(3)
+    far_block(5)
+    peer_block(4)
+    far_block(4)
 
     vc8 = jnp.broadcast_to(vc.astype(F32), (8, NX * PER_X)).astype(BF)
     sel8 = jnp.broadcast_to(sel_ref[...].astype(F32), (8, SLOTS)).astype(BF)
@@ -255,8 +267,7 @@
     def values_of(r):
         return kv[pl.ds(chunk_of(r) * PER_X, PER_X), :, HEAD:KV].reshape(CHUNK, HEAD)
 
-    top = jnp.full((QROWS, 1), NEG, F32)
-    for r in range(NX):
+    def score(r):
         shard = chunk_of(r) * PER_X + lax.broadcasted_iota(
             jnp.int32, (NX * PER_X, CHUNK), 1
         ) // SLOTS
@@ -271,7 +282,20 @@
         scores = dot(queries, keys_of(r), 1, 1) * SCALE
         scores = jnp.where(place <= qpos_all, scores, NEG)
         s_ref[:, r * CHUNK:(r + 1) * CHUNK] = scores
-        top = jnp.maximum(top, jnp.max(scores, axis=1, keepdims=True))
+        return jnp.max(scores, axis=1, keepdims=True)
+
+    top = score(0)
+    for d in NEAREST:
+        zs = (z + NZ - d) % NZ
+        arrived(one(left, zs, y), ag_recv.at[0, d], to_left)
+        arrived(one(right, zs, y), ag_recv.at[1, d], to_right)
+        arrived(one(left, zs, 1 - y), ag_recv.at[2, d], to_left)
+        arrived(one(right, zs, 1 - y), ag_recv.at[3, d], to_right)
+    top = jnp.maximum(top, score(1))
+    top = jnp.maximum(top, score(3))
+    for d in NEAREST:
+        arrived(one(far, (z + NZ - d) % NZ, 1 - y), ag_recv.at[5, d], xpeer(2, 1))
+    top = jnp.maximum(top, score(2))
     norm = jnp.zeros((QROWS, 1), F32)
     for r in range(NX):
         terms = jnp.exp(s_ref[:, r * CHUNK:(r + 1) * CHUNK] - top)
@@ -307,15 +331,19 @@
     for d in FARTHEST:
         zt = (z + d) % NZ
         send(tb.at[0, zt, 1 - y], hy.at[zt], rs_send.at[0, d], rs_recv.at[0, d], to_y)
+    def near(d, k):
+        zt = (z + d) % NZ
+        if k == 1:
+            send(tb.at[1, zt], nl.at[zt], rs_send.at[1, d], rs_recv.at[1, d], to_right)
+        else:
+            send(tb.at[2, zt], nr.at[zt], rs_send.at[2, d], rs_recv.at[2, d], to_left)
+
     for k, r in ((1, 1), (2, 3)):
         dq, kt, vt = column(r, dq)
         tb[k, :, :, :, 0:HEAD] = kt.astype(BF)
         tb[k, :, :, :, HEAD:KV] = vt.astype(BF)
-
-    def near(d):
-        zt = (z + d) % NZ
-        send(tb.at[1, zt], nl.at[zt], rs_send.at[1, d], rs_recv.at[1, d], to_right)
-        send(tb.at[2, zt], nr.at[zt], rs_send.at[2, d], rs_recv.at[2, d], to_left)
+        for d in FARTHEST[:3]:
+            near(d, k)
 
     def distant(d):
         zt = (z + d) % NZ
@@ -323,15 +351,14 @@
         fb[zt] = (tf2[zt, y] + hy[zt].astype(F32)).astype(BF)
         send(fb.at[zt], fx.at[zt], rs_send.at[3, d], rs_recv.at[3, d], to_far)
 
-    for d in FARTHEST[:3]:
-        near(d)
     dq, kt, vt = column(0, dq)
     tf[:, :, :, 0:HEAD] = kt
     tf[:, :, :, HEAD:KV] = vt
     for d in FARTHEST[:3]:
         distant(d)
     for d in FARTHEST[3:]:
-        near(d)
+        near(d, 1)
+        near(d, 2)
         distant(d)
     for h in range(HEADS):
         dq_ref[:, h * HEAD:(h + 1) * HEAD] = dq[h * SLOTS:(h + 1) * SLOTS].astype(BF)
@@ -487,10 +514,10 @@
     att, dq, rows, wgr = pl.pallas_call(
         kernel,
         out_shape=(
-            shape((SLOTS, HEADS * HEAD), BF),
-            shape((SLOTS, HEADS * HEAD), BF),
-            shape((SLOTS, MODEL // 4), BF),
-            shape((HEAD, KV), BF),
+            V((SLOTS, HEADS * HEAD), BF),
+            V((SLOTS, HEADS * HEAD), BF),
+            V((SLOTS, MODEL // 4), BF),
+            V((HEAD, KV), BF),
         ),
         in_specs=[pl.BlockSpec(memory_space=pl.ANY)] * 7,
         out_specs=(vmem,) * 4,

time: 87.1 us -> 79.5 us (0.913)
  Pallas kernels: 82.7 us -> 78.7 us
  local copies, waits for them, and re-layouts: 3.42 us -> 0.01 us
    pallas_call x1, Pallas kernels: 81.4 us -> 77.3 us  [local(): pl.pallas_call(kernel, out_shape=(V((SLOTS, HEADS * HEAD), BF), V((SLOTS,...]
    unnamed x10 -> x2, local copies, waits for them, and re-layouts: 3.42 us -> 0.01 us
where the time goes in v3:
time: 79.5 us; the launch traced here: 79.4 us
  Pallas kernels  78.7 us (99%)
    pallas_call x1, Pallas kernels, local(): pl.pallas_call(kernel, out_shape=(V((SLOTS, HEADS * HEAD), BF), V((SLOTS,...  77.3 us

profile of v3, /device:TPU:8, one launch (start us, length us, event | category | flops | bytes accessed | tf_op | source)
XLA Modules:
  0.0 79.4 jit_solution(17932091177115611132)
XLA Ops:
  0.6 0.0 copy-start
  0.6 77.3 %shard_map.110 = (bf16[32,1024]{1,0:T(8,128)(2,1)S(1)}, bf16[32,1024]{1,0:T(8,128)(2,1)S(1)}, bf16[32,2048]{1,0:T(8,128)(2,1)S(1)}, bf16[128,256]{1,0:T(8,128)(2,1)S(1)}) custom-call(bf16[256,8192]{1,0:T(8,128)(2,1)} %tok_hbm.1, s32[1,32]{1,0:T(1,128)} %bitcast.2, s32[1,64]{1,0:T(1,128)} %bitcast.4, bf16[32,1024]{1,0:T(8,128)(2,1)} %q_hbm.1, ...), custom_call_target="tpu_custom_call" | custom-call | tf_op jit(solution)/shard_map/pallas_call | solution.py:514
  78.0 0.0 copy-done
  78.0 1.4 %shard_map.111 = (bf16[32,1024]{1,0:T(8,128)(2,1)}, bf16[32,1024]{1,0:T(8,128)(2,1)}, bf16[256,2048]{1,0:T(8,128)(2,1)}, bf16[128,128]{1,0:T(8,128)(2,1)}, bf16[128,128]{1,0:T(8,128)(2,1)}) custom-call(s32[1,32]{1,0:T(1,128)S(1)} %bitcast.3, bf16[32,1024]{1,0:T(8,128)(2,1)S(1)} %get-tuple-element.9.att_in, bf16[32,1024]{1,0:T(8,128)(2,1)S(1)} %get-tuple-element.10.dq_in, ...), custom_call_target="tpu_custom_call" | custom-call | tf_op jit(solution)/shard_map/pallas_call | solution.py:529
Async XLA Ops:
  0.6 77.3 %copy-start = (s32[32]{0:T(128)S(1)}, s32[32]{0:T(128)}, u32[]{:S(2)}) copy-start(s32[32]{0:T(128)} %param.8) | copy-start | bytes 388

commit v4 on v3

--- a/solution.py
+++ b/solution.py
@@ -37,7 +37,7 @@
     att_ref, dq_ref, rows_ref, wgr_ref,
     tok, sel_ref, vc_ref, q_ref, g_ref, pz, xz, wg, pf, pk, pv, rk, rv, kv, s_ref, qs, gs,
     tf, tf2, tb, hy, fb, fx, nl, nr, ub, zr, gz,
-    wb, wf, wx, rsb, rsr, rf, ryb, ryr, tz, tr,
+    wb, wf, wf2, why, wfb, wfx, wnl, wnr, wyb, wyr, rsb, rsr, rf, tz, tr,
     in_sem, w_send, w_recv, z_send, z_recv, x_send, x_recv, ag_send, ag_recv, rs_send, rs_recv,
     t_send, t_recv,
 ):
@@ -71,8 +71,10 @@
     to_left = at(left, z, y)
     to_far = at(far, z, y)
     to_y = at(x, z, 1 - y)
+    def zpeer_ylo(d):
+        return {"ctx": (x * NZ + (z + d) % NZ) * NY + y, "tp": 2 * (1 - ylo) + core}
+
     to_sib = {"ctx": c, "tp": 2 * ylo + 1 - core}
-    to_ylo = {"ctx": c, "tp": 2 * (1 - ylo) + core}
 
     started = []
 
@@ -92,7 +94,8 @@
 
     barrier = pltpu.get_barrier_semaphore()
     partners = [zpeer(d) for d in range(1, NZ)] + [zpeer_y(d) for d in range(1, NZ)]
-    partners += [xpeer(r, k) for r in range(1, NX) for k in range(2)] + [to_y, to_sib, to_ylo]
+    partners += [xpeer(r, k) for r in range(1, NX) for k in range(2)] + [to_y, to_sib]
+    partners += [zpeer_ylo(d) for d in range(NZ)]
     for dev in partners:
         pl.semaphore_signal(barrier, inc=1, device_id=dev, device_id_type=pl.DeviceIdType.MESH)
 
@@ -404,40 +407,45 @@
     for d in FARTHEST:
         zt = (z + d) % NZ
         send(rsb.at[zt], rsr.at[zt], t_send.at[1, d], t_recv.at[1, d], to_sib)
-    for r in (2, 1, 3):
-        wb[r] = weight_part(r).astype(BF)
-        for k in (1, 0):
-            send(wb.at[r, half_of(k)], wx.at[r, k], x_send.at[r, k], x_recv.at[r, k], xpeer(r, k))
+    wf2[...] = weight_part(2)
+    wb[0] = wf2[...].astype(BF)
+    send(wb.at[0, 1 - y], why, x_send.at[0, 0], x_recv.at[0, 0], to_y)
+    wb[1] = weight_part(1).astype(BF)
+    send(wb.at[1], wnl, x_send.at[1, 0], x_recv.at[1, 0], to_right)
+    wb[2] = weight_part(3).astype(BF)
+    send(wb.at[2], wnr, x_send.at[2, 0], x_recv.at[2, 0], to_left)
     for k in range(2):
         rf[:, k] = row_part(2 * k + core)
     for d in FARTHEST:
         zt = (z + d) % NZ
         arrived(rsr.at[zt], t_recv.at[1, d], to_sib)
-        ryb[zt] = (rf[zt, 1 - ylo] + rsr[zt, 1 - ylo].astype(F32)).astype(BF)
-        send(ryb.at[zt], ryr.at[zt], t_send.at[2, d], t_recv.at[2, d], to_ylo)
+        tz[zt] = (rf[zt] + rsr[zt].astype(F32)).astype(BF)
+        send(tz.at[zt, 1 - ylo], tr.at[z, 1], t_send.at[2, d], t_recv.at[2, d], zpeer_ylo(d))
+        if d:
+            send(tz.at[zt, ylo], tr.at[z, 0], t_send.at[3, d], t_recv.at[3, d], zpeer(d))
+    tr[z, 0] = tz[z, ylo]
     wf[...] = weight_part(0)
-    wb[0] = wf[...].astype(BF)
-    send(wb.at[0, 1 - y], wx.at[0, 1], x_send.at[0, 1], x_recv.at[0, 1], to_y)
-    for d in FARTHEST:
-        zt = (z + d) % NZ
-        arrived(ryr.at[zt], t_recv.at[2, d], to_ylo)
-        tz[zt] = (
-            rf[zt, ylo] + rsr[zt, ylo].astype(F32) + ryr[zt].astype(F32)
-        ).astype(BF)
+    arrived(why, x_recv.at[0, 0], to_y)
+    wfb[...] = (wf2[y] + why[...].astype(F32)).astype(BF)
+    send(wfb, wfx, x_send.at[3, 0], x_recv.at[3, 0], to_far)
+    arrived(wnl, x_recv.at[1, 0], to_left)
+    arrived(wnr, x_recv.at[2, 0], to_right)
+    wf[...] = wf[...] + wnl[...].astype(F32) + wnr[...].astype(F32)
+    wyb[...] = wf[1 - y].astype(BF)
+    send(wyb, wyr, x_send.at[0, 1], x_recv.at[0, 1], to_y)
+
+    for d in NEAREST:
+        zs = (z + NZ - d) % NZ
+        arrived(tr.at[zs, 1], t_recv.at[2, d], zpeer_ylo(d))
         if d:
-            send(tz.at[zt], tr.at[z], t_send.at[3, d], t_recv.at[3, d], zpeer(d))
-    tr[z] = tz[z]
-    for d in ARRIVE:
-        zs = (z + NZ - d) % NZ
-        arrived(tr.at[zs], t_recv.at[3, d], zpeer(d))
+            arrived(tr.at[zs, 0], t_recv.at[3, d], zpeer(d))
     for zs in range(NZ):
-        rows_ref[:, zs * KV:(zs + 1) * KV] = (tr[zs].astype(F32) * live).astype(BF)
-
-    total = wf[y]
-    for r, k in XORDER:
-        arrived(wx.at[r, k], x_recv.at[r, k], xpeer(NX - r, k))
-        total = total + wx[r, k].astype(F32)
-    wgr_ref[...] = total.astype(BF)
+        both = tr[zs, 0].astype(F32) + tr[zs, 1].astype(F32)
+        rows_ref[:, zs * KV:(zs + 1) * KV] = (both * live).astype(BF)
+
+    arrived(wfx, x_recv.at[3, 0], to_far)
+    arrived(wyr, x_recv.at[0, 1], to_y)
+    wgr_ref[...] = (wf[y] + wfx[...].astype(F32) + wyr[...].astype(F32)).astype(BF)
 
     for cp in started:
         cp.wait_send()
@@ -496,16 +504,21 @@
         V(pairs, BF),
         V(pairs, BF),
         V(block, BF),
-        V((NX, NY, HEAD, KV), BF),
+        V((3, NY, HEAD, KV), BF),
         V((NY, HEAD, KV), F32),
-        V((NX, 2, HEAD, KV), BF),
+        V((NY, HEAD, KV), F32),
+        V((HEAD, KV), BF),
+        V((HEAD, KV), BF),
+        V((HEAD, KV), BF),
+        V((NY, HEAD, KV), BF),
+        V((NY, HEAD, KV), BF),
+        V((HEAD, KV), BF),
+        V((HEAD, KV), BF),
         V((NZ, 2, SLOTS, KV), BF),
         V((NZ, 2, SLOTS, KV), BF),
         V((NZ, 2, SLOTS, KV), F32),
-        V(block, BF),
-        V(block, BF),
-        V(block, BF),
-        V(block, BF),
+        V((NZ, 2, SLOTS, KV), BF),
+        V((NZ, 2, SLOTS, KV), BF),
         dma((8,)), dma((NX, 2)), dma((NX, 2)), dma((7, NZ)), dma((7, NZ)), dma((NX, 2)),
         dma((NX, 2)),
         dma((6, NZ)), dma((6, NZ)), dma((4, NZ)), dma((4, NZ)), dma((5, NZ)), dma((5, NZ)),

time: 79.5 us -> 78.3 us (0.985)
  Pallas kernels: 78.7 us -> 77.4 us
    pallas_call x1, Pallas kernels: 77.3 us -> 76 us  [local(): pl.pallas_call(kernel, out_shape=(V((SLOTS, HEADS * HEAD), BF), V((SLOTS,...]
where the time goes in v4:
time: 78.3 us; the launch traced here: 78.1 us
  Pallas kernels  77.4 us (99%)
    pallas_call x1, Pallas kernels, local(): pl.pallas_call(kernel, out_shape=(V((SLOTS, HEADS * HEAD), BF), V((SLOTS,...  76 us

profile of v4, /device:TPU:8, one launch (start us, length us, event | category | flops | bytes accessed | tf_op | source)
XLA Modules:
  0.0 78.1 jit_solution(17403332287259480033)
XLA Ops:
  0.6 0.0 copy-start
  0.6 76.0 %shard_map.110 = (bf16[32,1024]{1,0:T(8,128)(2,1)S(1)}, bf16[32,1024]{1,0:T(8,128)(2,1)S(1)}, bf16[32,2048]{1,0:T(8,128)(2,1)S(1)}, bf16[128,256]{1,0:T(8,128)(2,1)S(1)}) custom-call(bf16[256,8192]{1,0:T(8,128)(2,1)} %tok_hbm.1, s32[1,32]{1,0:T(1,128)} %bitcast.2, s32[1,64]{1,0:T(1,128)} %bitcast.4, bf16[32,1024]{1,0:T(8,128)(2,1)} %q_hbm.1, ...), custom_call_target="tpu_custom_call" | custom-call | tf_op jit(solution)/shard_map/pallas_call | solution.py:527
  76.7 0.0 copy-done
  76.7 1.4 %shard_map.111 = (bf16[32,1024]{1,0:T(8,128)(2,1)}, bf16[32,1024]{1,0:T(8,128)(2,1)}, bf16[256,2048]{1,0:T(8,128)(2,1)}, bf16[128,128]{1,0:T(8,128)(2,1)}, bf16[128,128]{1,0:T(8,128)(2,1)}) custom-call(s32[1,32]{1,0:T(1,128)S(1)} %bitcast.3, bf16[32,1024]{1,0:T(8,128)(2,1)S(1)} %get-tuple-element.9.att_in, bf16[32,1024]{1,0:T(8,128)(2,1)S(1)} %get-tuple-element.10.dq_in, ...), custom_call_target="tpu_custom_call" | custom-call | tf_op jit(solution)/shard_map/pallas_call | solution.py:542
Async XLA Ops:
  0.6 76.1 %copy-start = (s32[32]{0:T(128)S(1)}, s32[32]{0:T(128)}, u32[]{:S(2)}) copy-start(s32[32]{0:T(128)} %param.8) | copy-start | bytes 388

commit v5 on v4

--- a/solution.py
+++ b/solution.py
@@ -89,6 +89,11 @@
         cp.start()
         started.append(cp)
 
+    def drain(count):
+        for cp in started[:count]:
+            cp.wait_send()
+        del started[:count]
+
     def arrived(dst, rsem, dev):
         copy(dst, dst, rsem, rsem, dev).wait_recv()
 
@@ -177,6 +182,7 @@
         acc = acc + dot(
             xz[xx].reshape(NZ * SLOTS, KV), wg[xx].reshape(NY * HEAD, KV), 1, 0
         )
+    earlier = len(started)
     pf[...] = acc.reshape(NZ, SLOTS, KV)
     pk[...] = pf[:, :, 0:HEAD]
     pv[...] = pf[:, :, HEAD:KV].astype(BF)
@@ -184,6 +190,7 @@
         zt = (z + d) % NZ
         send(pk.at[zt], rk.at[z], z_send.at[2, d], z_recv.at[2, d], zpeer(d))
         send(pv.at[zt], rv.at[z], t_send.at[4, d], t_recv.at[4, d], zpeer(d))
+    drain(earlier)
     key_sum = pf[z, :, 0:HEAD]
     value_sum = pf[z, :, HEAD:KV]
     for d in ARRIVE:
@@ -316,6 +323,7 @@
         att_ref[:, h * HEAD:(h + 1) * HEAD] = attended[h * SLOTS:(h + 1) * SLOTS]
     out_dot = jnp.sum(grads.astype(F32) * attended.astype(F32), axis=1, keepdims=True)
 
+    earlier = len(started)
     dq = jnp.zeros((QROWS, HEAD), F32)
 
     def column(r, dq):
@@ -376,6 +384,7 @@
         if d:
             send(ub.at[zt, y], zr.at[z, y], z_send.at[4, d], z_recv.at[4, d], zpeer(d))
         send(ub.at[zt, 1 - y], zr.at[z, y], t_send.at[0, d], t_recv.at[0, d], zpeer_y(d))
+    drain(earlier)
     total = tf[z, y]
     arrived(zr.at[z, 1 - y], t_recv.at[0, 0], to_y)
     total = total + zr[z, 1 - y].astype(F32)
@@ -386,8 +395,11 @@
         total = total + zr[zs, y].astype(F32) + zr[zs, 1 - y].astype(F32)
     gz[z] = total.astype(BF)
 
+    earlier = len(started)
     for d in ZORDER:
         send(gz.at[z], gz.at[z], z_send.at[5, d], z_recv.at[5, d], zpeer(d))
+    drain(earlier)
+    earlier = len(started)
     for d in ARRIVE:
         zs = (z + NZ - d) % NZ
         arrived(gz.at[zs], z_recv.at[5, d], zpeer(d))
@@ -434,6 +446,8 @@
     wyb[...] = wf[1 - y].astype(BF)
     send(wyb, wyr, x_send.at[0, 1], x_recv.at[0, 1], to_y)
 
+    drain(earlier)
+
     for d in NEAREST:
         zs = (z + NZ - d) % NZ
         arrived(tr.at[zs, 1], t_recv.at[2, d], zpeer_ylo(d))
@@ -447,8 +461,7 @@
     arrived(wyr, x_recv.at[0, 1], to_y)
     wgr_ref[...] = (wf[y] + wfx[...].astype(F32) + wyr[...].astype(F32)).astype(BF)
 
-    for cp in started:
-        cp.wait_send()
+    drain(len(started))
 
 
 def finish(

time: 78.3 us -> 78.1 us (level)
  no operation moved by 1% of the time
where the time goes in v5:
time: 78.1 us; the launch traced here: 77.8 us
  Pallas kernels  77.2 us (99%)
    pallas_call x1, Pallas kernels, local(): pl.pallas_call(kernel, out_shape=(V((SLOTS, HEADS * HEAD), BF), V((SLOTS,...  75.8 us

profile of v5, /device:TPU:8, one launch (start us, length us, event | category | flops | bytes accessed | tf_op | source)
XLA Modules:
  0.0 77.8 jit_solution(1612408225262298072)
XLA Ops:
  0.6 0.0 copy-start
  0.6 75.8 %shard_map.110 = (bf16[32,1024]{1,0:T(8,128)(2,1)S(1)}, bf16[32,1024]{1,0:T(8,128)(2,1)S(1)}, bf16[32,2048]{1,0:T(8,128)(2,1)S(1)}, bf16[128,256]{1,0:T(8,128)(2,1)S(1)}) custom-call(bf16[256,8192]{1,0:T(8,128)(2,1)} %tok_hbm.1, s32[1,32]{1,0:T(1,128)} %bitcast.2, s32[1,64]{1,0:T(1,128)} %bitcast.4, bf16[32,1024]{1,0:T(8,128)(2,1)} %q_hbm.1, ...), custom_call_target="tpu_custom_call" | custom-call | tf_op jit(solution)/shard_map/pallas_call | solution.py:540
  76.4 0.0 copy-done
  76.5 1.4 %shard_map.111 = (bf16[32,1024]{1,0:T(8,128)(2,1)}, bf16[32,1024]{1,0:T(8,128)(2,1)}, bf16[256,2048]{1,0:T(8,128)(2,1)}, bf16[128,128]{1,0:T(8,128)(2,1)}, bf16[128,128]{1,0:T(8,128)(2,1)}) custom-call(s32[1,32]{1,0:T(1,128)S(1)} %bitcast.3, bf16[32,1024]{1,0:T(8,128)(2,1)S(1)} %get-tuple-element.9.att_in, bf16[32,1024]{1,0:T(8,128)(2,1)S(1)} %get-tuple-element.10.dq_in, ...), custom_call_target="tpu_custom_call" | custom-call | tf_op jit(solution)/shard_map/pallas_call | solution.py:555
Async XLA Ops:
  0.6 75.8 %copy-start = (s32[32]{0:T(128)S(1)}, s32[32]{0:T(128)}, u32[]{:S(2)}) copy-start(s32[32]{0:T(128)} %param.8) | copy-start | bytes 388
